TPU v7x, 256 devices: a whole 4x4x8 slice. The times are simulated.
256 devices in a mesh: dp: 32 (over x, z), fsdp: 8 (over y, core).
Axes of the slice: x: 4, y: 4, z: 8, core: 2. Of those that a mesh axis runs over, the one named last changes fastest.
Arguments:
- hidden: bfloat16 [8192, 28672], P('dp', 'fsdp'), may hold values from -6 to 6
- cotangent: bfloat16 [8192, 8192], P('dp', 'fsdp'), may hold values from -6 to 6
- region_ids: int32 [8192], P('dp'), may hold values from 0 to 255, as said below
- adapter_a: bfloat16 [256, 64, 28672], P('dp', None, 'fsdp'), may hold values from -0.03125 to 0.03125
- adapter_b: bfloat16 [256, 64, 8192], P('dp', None, 'fsdp'), may hold values from -0.75 to 0.75
Outputs:
- grad_a: bfloat16 [256, 64, 28672], P('dp', None, 'fsdp')
- grad_b: bfloat16 [256, 64, 8192], P('dp', None, 'fsdp')
- grad_hidden: bfloat16 [8192, 28672], P('dp', 'fsdp')
Inputs may be any that keep to these rules, and one draw needn't show every extreme that they name: `region_ids`: region r belongs to owner r // 8. In each aligned block of 256 tokens (the tokens of one index of dp) the ids never fall, and at most 24 tokens name regions of one owner; in every block 4 owners, the same ones in every block, reach that bound.
All inputs are finite; a program needn't handle non-finite values.
Results may differ from a plain program's by a relative error of at most 0.0049.
Values may be sent and summed in bfloat16 or wider, within the bound.
A program may use at most 128 MiB of HBM per device.

v0:
```python
import jax
import jax.numpy as jnp
from jax import lax
from jax.sharding import PartitionSpec as P


def contract_rows(left, right):
    return lax.dot_general(
        left, right, (((0,), (0,)), ((), ())), preferred_element_type=jnp.float32
    )


def contract_cols(left, right):
    return lax.dot_general(
        left, right, (((1,), (1,)), ((), ())), preferred_element_type=jnp.float32
    )


def shards(hidden, cotangent, region_ids, adapter_a, adapter_b):
    owner_count = lax.axis_size("dp")
    token_count = hidden.shape[0]
    local_count = adapter_a.shape[0]
    rank_width = adapter_a.shape[1]
    hidden_width = hidden.shape[1]
    model_width = cotangent.shape[1]
    capacity = 3 * token_count // owner_count
    owner_of = region_ids // local_count
    owner_ids = jnp.arange(owner_count, dtype=jnp.int32)
    counts = jnp.sum((owner_of[:, None] == owner_ids[None, :]).astype(jnp.int32), axis=0)
    starts = jnp.cumsum(counts) - counts
    slot_index = jnp.arange(capacity, dtype=jnp.int32)
    usable = slot_index[None, :] < counts[:, None]
    row_index = jnp.where(usable, starts[:, None] + slot_index[None, :], 0)
    send_hidden = jnp.where(usable[:, :, None], hidden[row_index], jnp.zeros((), jnp.bfloat16))
    send_cotangent = jnp.where(
        usable[:, :, None], cotangent[row_index], jnp.zeros((), jnp.bfloat16)
    )
    send_local = jnp.where(usable, region_ids[row_index] % local_count, local_count).astype(
        jnp.bfloat16
    )
    recv_hidden, recv_cotangent, recv_local = (
        lax.all_to_all(send_hidden, "dp", split_axis=0, concat_axis=0, tiled=True),
        lax.all_to_all(send_cotangent, "dp", split_axis=0, concat_axis=0, tiled=True),
        lax.all_to_all(send_local, "dp", split_axis=0, concat_axis=0, tiled=True),
    )
    total_rows = owner_count * capacity
    got_hidden = recv_hidden.reshape(total_rows, hidden_width)
    got_cotangent = recv_cotangent.reshape(total_rows, model_width)
    got_local = recv_local.reshape(total_rows)
    local_ids = jnp.arange(local_count).astype(jnp.bfloat16)
    onehot = (got_local[:, None] == local_ids[None, :]).astype(jnp.float32)
    flat_a = adapter_a.reshape(local_count * rank_width, hidden_width)
    flat_b = adapter_b.reshape(local_count * rank_width, model_width)
    part_down = contract_cols(got_hidden, flat_a)
    part_back = contract_cols(got_cotangent, flat_b)
    full_down, full_back = lax.psum((part_down, part_back), "fsdp")
    column_mask = jnp.repeat(onehot, rank_width, axis=1)
    down_rows = (full_down * column_mask).astype(jnp.bfloat16)
    back_rows = (full_back * column_mask).astype(jnp.bfloat16)
    grad_b = (
        contract_rows(down_rows, got_cotangent)
        .reshape(local_count, rank_width, model_width)
        .astype(jnp.bfloat16)
    )
    grad_a = (
        contract_rows(back_rows, got_hidden)
        .reshape(local_count, rank_width, hidden_width)
        .astype(jnp.bfloat16)
    )
    returned = jnp.dot(back_rows, flat_a, preferred_element_type=jnp.float32).astype(jnp.bfloat16)
    returned = returned.reshape(owner_count, capacity, hidden_width)
    arrived = lax.all_to_all(returned, "dp", split_axis=0, concat_axis=0, tiled=True)
    position = jnp.arange(token_count, dtype=jnp.int32) - starts[owner_of]
    grad_hidden = arrived[owner_of, position]
    return (grad_a, grad_b, grad_hidden)


def solution(mesh):
    return jax.shard_map(
        shards,
        mesh=mesh,
        in_specs=(
            P("dp", "fsdp"),
            P("dp", "fsdp"),
            P("dp"),
            P("dp", None, "fsdp"),
            P("dp", None, "fsdp"),
        ),
        out_specs=(P("dp", None, "fsdp"), P("dp", None, "fsdp"), P("dp", "fsdp")),
        check_vma=False,
    )
```

profile of v0, /device:TPU:113, one launch (start us, length us, event | category | flops | bytes accessed | tf_op | source)
XLA Modules:
  0.0 435.8 jit_solution(75697185103851389)
XLA Ops:
  8.7 4.9 %gather_fusion = bf16[768,1024]{1,0:T(8,128)(2,1)S(1)} fusion(bf16[256,1024]{1,0:T(8,128)(2,1)} %param.6, s32[1024]{0:T(1024)S(1)} %pad_clamp_fusion), kind=kCustom, calls=%fused_computation | custom fusion | bytes 3148800 | tf_op jit(solution)/shard_map/gather | solution.py:36
  13.6 1.3 broadcast_select_fusion.1
  14.9 9.7 %all-to-all-start = ((bf16[32,24,1024]{2,1,0:T(8,128)(2,1)}), bf16[32,24,1024]{2,1,0:T(8,128)(2,1)S(1)}, u32[]{:S(2)}, u32[]{:S(2)}) async-start(bf16[32,24,1024]{2,1,0:T(8,128)(2,1)} %broadcast_select_fusion.1), calls=%async_computation | async-start | bytes 3145728 | tf_op jit(solution)/shard_map/all_to_all | solution.py:43
  24.7 5.4 %gather_fusion.2 = bf16[768,3584]{1,0:T(8,128)(2,1)} fusion(bf16[256,3584]{1,0:T(8,128)(2,1)S(1)} %copy-done, s32[1024]{0:T(1024)S(1)} %pad_clamp_fusion), kind=kCustom, calls=%fused_computation.2 | custom fusion | bytes 11013120 | tf_op jit(solution)/shard_map/gather | solution.py:34
  30.1 5.5 %broadcast_select_fusion = bf16[32,24,3584]{2,1,0:T(8,128)(2,1)} fusion(bf16[32,24,3584]{2,1,0:T(8,128)(2,1)} %bitcast.65, pred[32,24]{1,0:T(8,128)(4,1)S(1)} %iota_compare_fusion.2), kind=kLoop, calls=%fused_computation.6 | loop fusion | flops 2752512 | bytes 11010816 | tf_op jit(solution)/shard_map/jit(_where)/select_n | solution.py:34
  35.5 26.7 %all-to-all-done = bf16[32,24,1024]{2,1,0:T(8,128)(2,1)S(1)} async-done(((bf16[32,24,1024]{2,1,0:T(8,128)(2,1)}), bf16[32,24,1024]{2,1,0:T(8,128)(2,1)S(1)}, u32[]{:S(2)}, u32[]{:S(2)}) %all-to-all-start) | async-done | bytes 1572896 | tf_op jit(solution)/shard_map/all_to_all | solution.py:43
  62.2 6.9 %all-to-all-start.2 = ((bf16[32,24,3584]{2,1,0:T(8,128)(2,1)}), bf16[32,24,3584]{2,1,0:T(8,128)(2,1)}, u32[]{:S(2)}, u32[]{:S(2)}) async-start(bf16[32,24,3584]{2,1,0:T(8,128)(2,1)} %broadcast_select_fusion), calls=%async_computation.2 | async-start | bytes 11010048 | tf_op jit(solution)/shard_map/all_to_all | solution.py:42
  69.2 3.4 fusion.9
  72.6 117.1 %all-to-all-done.2 = bf16[32,24,3584]{2,1,0:T(8,128)(2,1)} async-done(((bf16[32,24,3584]{2,1,0:T(8,128)(2,1)}), bf16[32,24,3584]{2,1,0:T(8,128)(2,1)}, u32[]{:S(2)}, u32[]{:S(2)}) %all-to-all-start.2) | async-done | bytes 5505056 | tf_op jit(solution)/shard_map/all_to_all | solution.py:42
  189.7 7.8 %fusion.10 = f32[768,512]{1,0:T(8,128)} fusion(bf16[768,3584]{1,0:T(8,128)(2,1)} %bitcast.8, bf16[512,3584]{1,0:T(8,128)(2,1)} %bitcast.78), kind=kOutput, calls=%fused_computation.71 | convolution fusion | flops 2818572288 | bytes 10747904 | tf_op jit(solution)/shard_map/dot_general | solution.py:14
  198.2 5.0 %gather_fusion.1 = s32[768]{0:T(1024)S(1)} fusion(s32[256]{0:T(256)S(1)} %copy-done.1, s32[1024]{0:T(1024)S(1)} %pad_clamp_fusion), kind=kCustom, calls=%fused_computation.1 | custom fusion | bytes 9216 | tf_op jit(solution)/shard_map/gather | solution.py:38
  204.0 10.4 %all-to-all-start.1 = ((bf16[32,1,24]{2,1,0:T(2,128)(2,1)}), bf16[32,1,24]{2,1,0:T(2,128)(2,1)S(1)}, u32[]{:S(2)}, u32[]{:S(2)}) async-start(bf16[32,1,24]{2,1,0:T(2,128)(2,1)} %copy.32), calls=%async_computation.1 | async-start | bytes 32768 | tf_op jit(solution)/shard_map/all_to_all | solution.py:44
  214.5 5.9 %all-to-all-done.1 = bf16[32,1,24]{2,1,0:T(2,128)(2,1)S(1)} async-done(((bf16[32,1,24]{2,1,0:T(2,128)(2,1)}), bf16[32,1,24]{2,1,0:T(2,128)(2,1)S(1)}, u32[]{:S(2)}, u32[]{:S(2)}) %all-to-all-start.1) | async-done | bytes 1568 | tf_op jit(solution)/shard_map/all_to_all | solution.py:44
  220.8 1.7 copy.33
  222.5 49.1 %all-reduce.3.cloned.1.call-done = (f32[768,512]{1,0:T(8,128)}, f32[768,512]{1,0:T(8,128)}) async-done(((f32[768,512]{1,0:T(8,128)}, f32[768,512]{1,0:T(8,128)}), (f32[768,512]{1,0:T(8,128)}, f32[768,512]{1,0:T(8,128)})) %all-reduce.3.cloned.1.call-update) | async-done | bytes 3145744 | tf_op jit(solution)/shard_map/psum | solution.py:56
  271.6 3.1 fusion
  275.0 4.7 %convolution_convert_fusion = bf16[768,3584]{1,0:T(8,128)(2,1)} fusion(bf16[768,512]{1,0:T(8,128)(2,1)S(1)} %get-tuple-element.8, bf16[512,3584]{1,0:T(8,128)(2,1)S(1)} %bitcast.79), kind=kOutput, calls=%fused_computation.4 | convolution fusion | flops 2821324800 | bytes 9961472 | tf_op jit(solution)/shard_map/dot_general | solution.py:70
  279.8 9.4 %all-to-all-start.3 = ((bf16[32,24,3584]{2,1,0:T(8,128)(2,1)}), bf16[32,24,3584]{2,1,0:T(8,128)(2,1)}, u32[]{:S(2)}, u32[]{:S(2)}) async-start(bf16[32,24,3584]{2,1,0:T(8,128)(2,1)} %bitcast.69), calls=%async_computation.3 | async-start | bytes 11010048 | tf_op jit(solution)/shard_map/all_to_all | solution.py:72
  290.6 20.0 %compare_select_fusion.3 = s32[256]{0:T(256)S(1)} fusion(s32[]{:T(128)} %bitcast.16, s32[]{:T(128)} %bitcast.17, s32[]{:T(128)} %bitcast.18, s32[]{:T(128)} %bitcast.19, s32[]{:T(128)} %bitcast.20, s32[]{:T(128)} %bitcast.21, s32[]{:T(128)} %bitcast.22, s32[]{:T(128)} %bitcast.23, s32[]{:T(128)} %bitcast.24, s32[]{:T(128)} %bitcast.25, s32[]{:T(128)} %bitcast.26, ...), kind=kLoop, calls=%fused_computation.28 | loop fusion | flops 16640 | bytes 2176 | tf_op jit(solution)/shard_map/gather | solution.py:73
  310.6 1.2 copy.36
  312.0 3.6 convolution_convert_fusion.2
  315.6 7.0 %convolution_convert_fusion.1 = bf16[8,64,3584]{2,1,0:T(8,128)(2,1)} fusion(bf16[8,64,768]{2,1,0:T(8,128)(2,1)S(1)} %bitcast.73, bf16[768,3584,1]{1,0,2:T(8,128)(2,1)} %bitcast.9), kind=kOutput, calls=%fused_computation.5 | convolution fusion | flops 2820407296 | bytes 9961472 | tf_op jit(solution)/shard_map/dot_general | solution.py:8
  322.6 99.4 %all-to-all-done.3 = bf16[32,24,3584]{2,1,0:T(8,128)(2,1)} async-done(((bf16[32,24,3584]{2,1,0:T(8,128)(2,1)}), bf16[32,24,3584]{2,1,0:T(8,128)(2,1)}, u32[]{:S(2)}, u32[]{:S(2)}) %all-to-all-start.3) | async-done | bytes 5505056 | tf_op jit(solution)/shard_map/all_to_all | solution.py:72
  422.0 6.9 %gather_fusion.3 = bf16[256,3584]{1,0:T(8,128)(2,1)} fusion(bf16[32,24,3584]{2,1,0:T(8,128)(2,1)} %all-to-all-done.3, s32[256]{0:T(256)S(1)} %bitcast.66), kind=kCustom, calls=%fused_computation.3 | custom fusion | bytes 3672064 | tf_op jit(solution)/shard_map/gather | solution.py:74
  (33 shorter events, 5.4 us)
Async XLA Ops:
  7.2 17.5 %copy-start = (bf16[256,3584]{1,0:T(8,128)(2,1)S(1)}, bf16[256,3584]{1,0:T(8,128)(2,1)}, u32[]{:S(2)}) copy-start(bf16[256,3584]{1,0:T(8,128)(2,1)} %param.5) | copy-start | bytes 5505028
  14.9 47.3 %all-to-all-start = ((bf16[32,24,1024]{2,1,0:T(8,128)(2,1)}), bf16[32,24,1024]{2,1,0:T(8,128)(2,1)S(1)}, u32[]{:S(2)}, u32[]{:S(2)}) async-start(bf16[32,24,1024]{2,1,0:T(8,128)(2,1)} %broadcast_select_fusion.1), calls=%async_computation | async-start | bytes 3145728 | tf_op jit(solution)/shard_map/all_to_all | solution.py:43
  62.2 7.0 %copy-start.2 = (bf16[32,24,1024]{2,1,0:T(8,128)(2,1)}, bf16[32,24,1024]{2,1,0:T(8,128)(2,1)S(1)}, u32[]{:S(2)}) copy-start(bf16[32,24,1024]{2,1,0:T(8,128)(2,1)S(1)} %all-to-all-done) | copy-start | bytes 4718596
  62.2 127.5 %all-to-all-start.2 = ((bf16[32,24,3584]{2,1,0:T(8,128)(2,1)}), bf16[32,24,3584]{2,1,0:T(8,128)(2,1)}, u32[]{:S(2)}, u32[]{:S(2)}) async-start(bf16[32,24,3584]{2,1,0:T(8,128)(2,1)} %broadcast_select_fusion), calls=%async_computation.2 | async-start | bytes 11010048 | tf_op jit(solution)/shard_map/all_to_all | solution.py:42
  69.2 202.4 %all-reduce.3.cloned.1.call-start = ((), (), s32[]{:S(2)}) async-start(), calls=%async_computation.4 | async-start | bytes 6291456 | tf_op jit(solution)/shard_map/psum | solution.py:56
  197.5 0.7 copy-start.1
  204.0 16.4 %all-to-all-start.1 = ((bf16[32,1,24]{2,1,0:T(2,128)(2,1)}), bf16[32,1,24]{2,1,0:T(2,128)(2,1)S(1)}, u32[]{:S(2)}, u32[]{:S(2)}) async-start(bf16[32,1,24]{2,1,0:T(2,128)(2,1)} %copy.32), calls=%async_computation.1 | async-start | bytes 32768 | tf_op jit(solution)/shard_map/all_to_all | solution.py:44
  271.6 3.5 copy-start.3
  279.8 142.3 %all-to-all-start.3 = ((bf16[32,24,3584]{2,1,0:T(8,128)(2,1)}), bf16[32,24,3584]{2,1,0:T(8,128)(2,1)}, u32[]{:S(2)}, u32[]{:S(2)}) async-start(bf16[32,24,3584]{2,1,0:T(8,128)(2,1)} %bitcast.69), calls=%async_computation.3 | async-start | bytes 11010048 | tf_op jit(solution)/shard_map/all_to_all | solution.py:72
Sparse Core Ops, SparseCore 0:
  197.7 73.8 all-reduce.2
where the time goes:
time: 437 us; the launch traced here: 436 us
  waiting for transfers between devices  298 us (68%)
  starting transfers between devices  36.5 us (8%)
  other arithmetic  31.4 us (7%)
  local copies, waits for them, and re-layouts  29 us (7%)
  matrix products  26.6 us (6%)
  between operations  14.2 us (3%)
    all_to_all x1, waiting for transfers between devices, shards(): lax.all_to_all(send_hidden, 'dp', split_axis=0, concat_axis=0, tiled=True)  117 us
    all_to_all x1, waiting for transfers between devices, shards(): lax.all_to_all(returned, 'dp', split_axis=0, concat_axis=0, tiled=True)  99.4 us
    psum x1, waiting for transfers between devices, shards(): full_down, full_back = lax.psum((part_down, part_back), 'fsdp')  49.1 us
    all_to_all x1, waiting for transfers between devices, shards(): lax.all_to_all(send_cotangent, 'dp', split_axis=0, concat_axis=0, tiled=T...  26.7 us
    gather x1, other arithmetic, shards(): position = jnp.arange(token_count, dtype=jnp.int32) - starts[owner_of]  20 us
    dot_general x2, matrix products, contract_cols(): lax.dot_general(left, right, (((1,), (1,)), ((), ())), preferred_element_...  11.2 us
    dot_general x2, matrix products, contract_rows(): lax.dot_general(left, right, (((0,), (0,)), ((), ())), preferred_element_...  10.6 us
    all_to_all x1, starting transfers between devices, shards(): lax.all_to_all(send_local, 'dp', split_axis=0, concat_axis=0, tiled=True)  10.4 us
  transfers between devices with their start and end apart: 5, of which 5 were waited for; matrix products, arithmetic and copies ran while one was open for 13% of the time, Pallas kernels for 0%

commit v1 on v0

--- a/solution.py
+++ b/solution.py
@@ -31,32 +31,38 @@
     slot_index = jnp.arange(capacity, dtype=jnp.int32)
     usable = slot_index[None, :] < counts[:, None]
     row_index = jnp.where(usable, starts[:, None] + slot_index[None, :], 0)
-    send_hidden = jnp.where(usable[:, :, None], hidden[row_index], jnp.zeros((), jnp.bfloat16))
-    send_cotangent = jnp.where(
-        usable[:, :, None], cotangent[row_index], jnp.zeros((), jnp.bfloat16)
-    )
+    id_width = 128
     send_local = jnp.where(usable, region_ids[row_index] % local_count, local_count).astype(
         jnp.bfloat16
     )
-    recv_hidden, recv_cotangent, recv_local = (
-        lax.all_to_all(send_hidden, "dp", split_axis=0, concat_axis=0, tiled=True),
-        lax.all_to_all(send_cotangent, "dp", split_axis=0, concat_axis=0, tiled=True),
-        lax.all_to_all(send_local, "dp", split_axis=0, concat_axis=0, tiled=True),
+    send = jnp.concatenate(
+        [
+            hidden[row_index],
+            cotangent[row_index],
+            jnp.broadcast_to(send_local[:, :, None], (owner_count, capacity, id_width)),
+        ],
+        axis=-1,
     )
+    recv = lax.all_to_all(send, "dp", split_axis=0, concat_axis=0, tiled=True)
     total_rows = owner_count * capacity
-    got_hidden = recv_hidden.reshape(total_rows, hidden_width)
-    got_cotangent = recv_cotangent.reshape(total_rows, model_width)
-    got_local = recv_local.reshape(total_rows)
+    recv = recv.reshape(total_rows, hidden_width + model_width + id_width)
+    got_hidden = recv[:, :hidden_width]
+    got_cotangent = recv[:, hidden_width : hidden_width + model_width]
+    got_local = recv[:, hidden_width + model_width]
     local_ids = jnp.arange(local_count).astype(jnp.bfloat16)
     onehot = (got_local[:, None] == local_ids[None, :]).astype(jnp.float32)
     flat_a = adapter_a.reshape(local_count * rank_width, hidden_width)
     flat_b = adapter_b.reshape(local_count * rank_width, model_width)
-    part_down = contract_cols(got_hidden, flat_a)
-    part_back = contract_cols(got_cotangent, flat_b)
-    full_down, full_back = lax.psum((part_down, part_back), "fsdp")
-    column_mask = jnp.repeat(onehot, rank_width, axis=1)
-    down_rows = (full_down * column_mask).astype(jnp.bfloat16)
-    back_rows = (full_back * column_mask).astype(jnp.bfloat16)
+    part_down = contract_cols(got_hidden, flat_a).reshape(total_rows, local_count, rank_width)
+    part_back = contract_cols(got_cotangent, flat_b).reshape(total_rows, local_count, rank_width)
+    pick_down = jnp.sum(part_down * onehot[:, :, None], axis=1)
+    pick_back = jnp.sum(part_back * onehot[:, :, None], axis=1)
+    full = lax.psum(jnp.concatenate([pick_down, pick_back], axis=1), "fsdp")
+    full_down = full[:, :rank_width].astype(jnp.bfloat16)
+    full_back = full[:, rank_width:].astype(jnp.bfloat16)
+    mask = onehot.astype(jnp.bfloat16)[:, :, None]
+    down_rows = (mask * full_down[:, None, :]).reshape(total_rows, local_count * rank_width)
+    back_rows = (mask * full_back[:, None, :]).reshape(total_rows, local_count * rank_width)
     grad_b = (
         contract_rows(down_rows, got_cotangent)
         .reshape(local_count, rank_width, model_width)
@@ -70,8 +76,9 @@
     returned = jnp.dot(back_rows, flat_a, preferred_element_type=jnp.float32).astype(jnp.bfloat16)
     returned = returned.reshape(owner_count, capacity, hidden_width)
     arrived = lax.all_to_all(returned, "dp", split_axis=0, concat_axis=0, tiled=True)
-    position = jnp.arange(token_count, dtype=jnp.int32) - starts[owner_of]
-    grad_hidden = arrived[owner_of, position]
+    before = jnp.sum((owner_of[None, :] < owner_of[:, None]).astype(jnp.int32), axis=1)
+    position = jnp.arange(token_count, dtype=jnp.int32) - before
+    grad_hidden = arrived.reshape(total_rows, hidden_width)[owner_of * capacity + position]
     return (grad_a, grad_b, grad_hidden)
 
 

time: 437 us -> 384 us (0.88); the launches traced: 436 us -> 377 us
  blocking collectives: 0 us -> 25 us
  other arithmetic: 31.4 us -> 7.57 us
  waiting for transfers between devices: 298 us -> 278 us
  starting transfers between devices: 36.5 us -> 17 us
  between operations: 14.2 us -> 0.81 us
  local copies, waits for them, and re-layouts: 29 us -> 23.7 us
    psum x1 -> x0, waiting for transfers between devices: 49.1 us -> none  [shards(): full_down, full_back = lax.psum((part_down, part_back), 'fsdp')]
    psum x0 -> x1, blocking collectives: none -> 25 us  [shards(): full = lax.psum(jnp.concatenate([pick_down, pick_back], axis=1), 'fsdp')]
    gather x2, other arithmetic: 20 us -> 0.01 us  [the longest x1 0.01 us: shards(): arrived.reshape(total_rows, hidden_width)[owner_of * capacity + position]]
    all_to_all x3 -> x1, starting transfers between devices: 27.1 us -> 9.9 us  [shards(): recv = lax.all_to_all(send, 'dp', split_axis=0, concat_axis=0, tiled=True)]
    all_to_all x1, waiting for transfers between devices: 99.4 us -> 114 us  [shards(): lax.all_to_all(returned, 'dp', split_axis=0, concat_axis=0, tiled=True)]
    all_to_all x3 -> x1, waiting for transfers between devices: 150 us -> 163 us  [shards(): recv = lax.all_to_all(send, 'dp', split_axis=0, concat_axis=0, tiled=True)]
    select_n x3, other arithmetic: 6.87 us -> 0.92 us  [the longest x1 0.83 us: shards(): owner_of = region_ids // local_count]
    concatenate x2, other arithmetic: 0.84 us -> 6.02 us  [the longest x1 5.99 us: shards(): jnp.concatenate([hidden[row_index], cotangent[row_index], jnp.broadcast_t...]
  transfers between devices with their start and end apart: 5 -> 2, of which waited for: 5 -> 2; matrix products, arithmetic and copies ran while one was open for 13% -> 3% of each run, Pallas kernels for 0% -> 0%
where the time goes in v1:
time: 384 us; the launch traced here: 377 us
  waiting for transfers between devices  278 us (72%)
  matrix products  25.3 us (7%)
  blocking collectives  25 us (7%)
  local copies, waits for them, and re-layouts  23.7 us (6%)
  starting transfers between devices  17 us (4%)
  other arithmetic  7.57 us (2%)
    all_to_all x1, waiting for transfers between devices, shards(): recv = lax.all_to_all(send, 'dp', split_axis=0, concat_axis=0, tiled=True)  163 us
    all_to_all x1, waiting for transfers between devices, shards(): lax.all_to_all(returned, 'dp', split_axis=0, concat_axis=0, tiled=True)  114 us
    psum x1, blocking collectives, shards(): full = lax.psum(jnp.concatenate([pick_down, pick_back], axis=1), 'fsdp')  25 us
    dot_general x2, matrix products, contract_rows(): lax.dot_general(left, right, (((0,), (0,)), ((), ())), preferred_element_...  10.4 us
    all_to_all x1, starting transfers between devices, shards(): recv = lax.all_to_all(send, 'dp', split_axis=0, concat_axis=0, tiled=True)  9.9 us
    dot_general x2, matrix products, contract_cols(): lax.dot_general(left, right, (((1,), (1,)), ((), ())), preferred_element_...  8.05 us
    gather x1, local copies, waits for them, and re-layouts, shards(): arrived.reshape(total_rows, hidden_width)[owner_of * capacity + position]  8.03 us
  transfers between devices with their start and end apart: 2, of which 2 were waited for; matrix products, arithmetic and copies ran while one was open for 3% of the time, Pallas kernels for 0%

profile of v1, /device:TPU:113, one launch (start us, length us, event | category | flops | bytes accessed | tf_op | source)
XLA Modules:
  0.0 376.8 jit_solution(14841344404088777715)
XLA Ops:
  0.7 0.8 and_select_fusion
  1.5 0.1 convert_reduce_fusion.1
  1.6 0.1 copy.10
  1.7 0.1 reduce
  1.9 0.1 reshape.240
  2.1 5.0 %gather_fusion.2 = s32[768]{0:T(1024)S(1)} fusion(s32[256]{0:T(256)S(1)} %copy-done.1, s32[1024]{0:T(1024)S(1)} %pad_clamp_fusion.1), kind=kCustom, calls=%fused_computation.2 | custom fusion | bytes 9216 | tf_op jit(solution)/shard_map/gather | solution.py:35
  7.1 0.1 reshape.255
  7.3 3.6 gather_fusion.1
  10.8 5.4 %gather_fusion = bf16[768,3584]{1,0:T(8,128)(2,1)} fusion(bf16[256,3584]{1,0:T(8,128)(2,1)S(1)} %copy-done, s32[1024]{0:T(1024)S(1)} %pad_clamp_fusion.1), kind=kCustom, calls=%fused_computation | custom fusion | bytes 11013120 | tf_op jit(solution)/shard_map/gather | solution.py:40
  16.2 0.2 broadcast_in_dim.10
  16.4 6.0 %pad_maximum_fusion = bf16[32,24,4736]{2,1,0:T(8,128)(2,1)} fusion(bf16[32,24,128]{2,1,0:T(8,128)(2,1)S(1)} %broadcast_in_dim.10, bf16[32,24,1024]{2,1,0:T(8,128)(2,1)S(1)} %bitcast.38, bf16[32,24,3584]{2,1,0:T(8,128)(2,1)} %bitcast.37), kind=kLoop, calls=%fused_computation.5 | loop fusion | flops 21823488 | bytes 14548992 | tf_op jit(solution)/shard_map/concatenate | solution.py:38
  22.4 9.9 %all-to-all-start = ((bf16[32,24,4736]{2,1,0:T(8,128)(2,1)}), bf16[32,24,4736]{2,1,0:T(8,128)(2,1)}, u32[]{:S(2)}, u32[]{:S(2)}) async-start(bf16[32,24,4736]{2,1,0:T(8,128)(2,1)} %pad_maximum_fusion), calls=%async_computation | async-start | bytes 14548992 | tf_op jit(solution)/shard_map/all_to_all | solution.py:46
  32.3 163.1 %all-to-all-done = bf16[32,24,4736]{2,1,0:T(8,128)(2,1)} async-done(((bf16[32,24,4736]{2,1,0:T(8,128)(2,1)}), bf16[32,24,4736]{2,1,0:T(8,128)(2,1)}, u32[]{:S(2)}, u32[]{:S(2)}) %all-to-all-start) | async-done | bytes 7274528 | tf_op jit(solution)/shard_map/all_to_all | solution.py:46
  195.4 1.2 slice_reduce_fusion
  196.7 2.4 multiply_reduce_fusion
  199.2 5.6 %multiply_reduce_fusion.1 = f32[768,64]{0,1:T(8,128)S(1)} fusion(bf16[8,64,3584]{2,1,0:T(8,128)(2,1)S(1)} %copy-done.4, bf16[768,4736]{1,0:T(8,128)(2,1)} %bitcast.3, f32[768,8]{0,1:T(8,128)S(1)} %get-tuple-element.6), kind=kOutput, calls=%fused_computation.11 | convolution fusion | flops 2819309568 | bytes 9396224 | tf_op jit(solution)/shard_map/dot_general | solution.py:14
  204.9 25.0 %all-reduce.1 = bf16[768,128]{0,1:T(8,128)(2,1)S(1)} all-reduce(f32[768,128]{0,1:T(8,128)S(1)} %pad_maximum_fusion.1), channel_id=1, replica_groups=mesh['dp'=32,'fsdp'=8] {'fsdp'}, use_global_device_ids=true, to_apply=%region_4.5 | all-reduce | flops 98304 | bytes 589824 | tf_op jit(solution)/shard_map/psum | solution.py:60
  229.8 6.9 %bitcast_convert_fusion = bf16[768,3584]{1,0:T(8,128)(2,1)} fusion(bf16[8,64,3584]{2,1,0:T(8,128)(2,1)} %param.8, bf16[768,64]{0,1:T(8,128)(2,1)S(1)} %get-tuple-element.4, bf16[768,8]{0,1:T(8,128)(2,1)S(1)} %get-tuple-element.5), kind=kOutput, calls=%fused_computation.4 | convolution fusion | flops 2821718016 | bytes 9285632 | tf_op jit(solution)/shard_map/dot_general | solution.py:76
  236.7 7.1 %all-to-all-start.1 = ((bf16[32,24,3584]{2,1,0:T(8,128)(2,1)}), bf16[32,24,3584]{2,1,0:T(8,128)(2,1)}, u32[]{:S(2)}, u32[]{:S(2)}) async-start(bf16[32,24,3584]{2,1,0:T(8,128)(2,1)} %bitcast.39), calls=%async_computation.1 | async-start | bytes 11010048 | tf_op jit(solution)/shard_map/all_to_all | solution.py:78
  243.8 0.2 convert_reduce_fusion
  244.0 3.4 convolution_convert_fusion.1
  247.3 7.0 %convolution_convert_fusion = bf16[8,64,3584]{2,1,0:T(8,128)(2,1)} fusion(bf16[768,4736]{1,0:T(8,128)(2,1)} %bitcast.3, bf16[768,64]{0,1:T(8,128)(2,1)S(1)} %get-tuple-element.4, bf16[768,8]{0,1:T(8,128)(2,1)S(1)} %get-tuple-element.5), kind=kOutput, calls=%fused_computation.6 | convolution fusion | flops 2820800512 | bytes 9285632 | tf_op jit(solution)/shard_map/dot_general | solution.py:8
  254.4 114.4 %all-to-all-done.1 = bf16[32,24,3584]{2,1,0:T(8,128)(2,1)} async-done(((bf16[32,24,3584]{2,1,0:T(8,128)(2,1)}), bf16[32,24,3584]{2,1,0:T(8,128)(2,1)}, u32[]{:S(2)}, u32[]{:S(2)}) %all-to-all-start.1) | async-done | bytes 5505056 | tf_op jit(solution)/shard_map/all_to_all | solution.py:78
  368.8 8.0 %gather_fusion.3 = bf16[256,3584]{1,0:T(8,128)(2,1)} fusion(bf16[768,3584]{1,0:T(8,128)(2,1)} %bitcast.14, s32[1024]{0:T(1024)S(1)} %pad_clamp_fusion), kind=kCustom, calls=%fused_computation.3 | custom fusion | bytes 3671040 | tf_op jit(solution)/shard_map/gather | solution.py:81
  (23 shorter events, 0.4 us)
Async XLA Ops:
  0.6 10.2 %copy-start = (bf16[256,3584]{1,0:T(8,128)(2,1)S(1)}, bf16[256,3584]{1,0:T(8,128)(2,1)}, u32[]{:S(2)}) copy-start(bf16[256,3584]{1,0:T(8,128)(2,1)} %param.5) | copy-start | bytes 5505028
  0.6 1.4 copy-start.1
  2.1 5.2 %copy-start.2 = (bf16[256,1024]{1,0:T(8,128)(2,1)S(1)}, bf16[256,1024]{1,0:T(8,128)(2,1)}, u32[]{:S(2)}) copy-start(bf16[256,1024]{1,0:T(8,128)(2,1)} %param.6) | copy-start | bytes 1572868
  10.8 5.6 %copy-start.3 = (bf16[768,1024]{1,0:T(8,128)(2,1)S(1)}, bf16[768,1024]{1,0:T(8,128)(2,1)}, u32[]{:S(2)}) copy-start(bf16[768,1024]{1,0:T(8,128)(2,1)} %gather_fusion.1) | copy-start | bytes 4718596
  22.4 174.3 %copy-start.5 = (bf16[8,64,1024]{2,1,0:T(8,128)(2,1)S(1)}, bf16[8,64,1024]{2,1,0:T(8,128)(2,1)}, u32[]{:S(2)}) copy-start(bf16[8,64,1024]{2,1,0:T(8,128)(2,1)} %param.9) | copy-start | bytes 3145732
  22.4 173.0 %all-to-all-start = ((bf16[32,24,4736]{2,1,0:T(8,128)(2,1)}), bf16[32,24,4736]{2,1,0:T(8,128)(2,1)}, u32[]{:S(2)}, u32[]{:S(2)}) async-start(bf16[32,24,4736]{2,1,0:T(8,128)(2,1)} %pad_maximum_fusion), calls=%async_computation | async-start | bytes 14548992 | tf_op jit(solution)/shard_map/all_to_all | solution.py:46
  195.4 3.8 copy-start.4
  236.7 132.1 %all-to-all-start.1 = ((bf16[32,24,3584]{2,1,0:T(8,128)(2,1)}), bf16[32,24,3584]{2,1,0:T(8,128)(2,1)}, u32[]{:S(2)}, u32[]{:S(2)}) async-start(bf16[32,24,3584]{2,1,0:T(8,128)(2,1)} %bitcast.39), calls=%async_computation.1 | async-start | bytes 11010048 | tf_op jit(solution)/shard_map/all_to_all | solution.py:78

commit v2 on v1

v2 whole, which is shorter than its diff:
```python
import jax
import jax.numpy as jnp
from jax import lax
from jax.sharding import PartitionSpec as P


def contract_rows(left, right):
    return lax.dot_general(
        left, right, (((0,), (0,)), ((), ())), preferred_element_type=jnp.float32
    )


def contract_cols(left, right):
    return lax.dot_general(
        left, right, (((1,), (1,)), ((), ())), preferred_element_type=jnp.float32
    )


def shards(hidden, cotangent, region_ids, adapter_a, adapter_b):
    owner_count = lax.axis_size("dp")
    token_count = hidden.shape[0]
    local_count = adapter_a.shape[0]
    rank_width = adapter_a.shape[1]
    hidden_width = hidden.shape[1]
    model_width = cotangent.shape[1]
    capacity = 3 * token_count // owner_count
    owner_of = region_ids // local_count
    owner_ids = jnp.arange(owner_count, dtype=jnp.int32)
    counts = jnp.sum((owner_of[:, None] == owner_ids[None, :]).astype(jnp.int32), axis=0)
    starts = jnp.cumsum(counts) - counts
    slot_index = jnp.arange(capacity, dtype=jnp.int32)
    usable = slot_index[None, :] < counts[:, None]
    row_index = jnp.where(usable, starts[:, None] + slot_index[None, :], token_count)
    id_width = 128
    table = jnp.concatenate(
        [
            hidden,
            cotangent,
            jnp.broadcast_to(
                (region_ids % local_count).astype(jnp.bfloat16)[:, None], (token_count, id_width)
            ),
        ],
        axis=-1,
    )
    flat_a = adapter_a.reshape(local_count * rank_width, hidden_width)
    flat_b = adapter_b.reshape(local_count * rank_width, model_width)
    local_ids = jnp.arange(local_count).astype(jnp.bfloat16)
    pieces = 2
    piece = capacity // pieces
    grad_a = None
    grad_b = None
    arrived = []
    for k in range(pieces):
        send = table.at[row_index[:, k * piece : (k + 1) * piece]].get(
            mode="fill", fill_value=local_count
        )
        recv = lax.all_to_all(send, "dp", split_axis=0, concat_axis=0, tiled=True)
        if k > 0:
            recv, full = lax.optimization_barrier((recv, full))
        rows = owner_count * piece
        recv = recv.reshape(rows, hidden_width + model_width + id_width)
        got_hidden = recv[:, :hidden_width]
        got_cotangent = recv[:, hidden_width : hidden_width + model_width]
        got_local = recv[:, hidden_width + model_width]
        onehot = (got_local[:, None] == local_ids[None, :]).astype(jnp.float32)
        part_down = contract_cols(got_hidden, flat_a).reshape(rows, local_count, rank_width)
        part_back = contract_cols(got_cotangent, flat_b).reshape(rows, local_count, rank_width)
        pick_down = jnp.sum(part_down * onehot[:, :, None], axis=1)
        pick_back = jnp.sum(part_back * onehot[:, :, None], axis=1)
        full = lax.psum(jnp.concatenate([pick_down, pick_back], axis=1), "fsdp")
        full_down = full[:, :rank_width].astype(jnp.bfloat16)
        full_back = full[:, rank_width:].astype(jnp.bfloat16)
        mask = onehot.astype(jnp.bfloat16)[:, :, None]
        down_rows = (mask * full_down[:, None, :]).reshape(rows, local_count * rank_width)
        back_rows = (mask * full_back[:, None, :]).reshape(rows, local_count * rank_width)
        returned = jnp.dot(back_rows, flat_a, preferred_element_type=jnp.float32).astype(
            jnp.bfloat16
        )
        returned = returned.reshape(owner_count, piece, hidden_width)
        arrived.append(lax.all_to_all(returned, "dp", split_axis=0, concat_axis=0, tiled=True))
        part_b = contract_rows(down_rows, got_cotangent)
        part_a = contract_rows(back_rows, got_hidden)
        grad_b = part_b if grad_b is None else grad_b + part_b
        grad_a = part_a if grad_a is None else grad_a + part_a
    grad_b = grad_b.reshape(local_count, rank_width, model_width).astype(jnp.bfloat16)
    grad_a = grad_a.reshape(local_count, rank_width, hidden_width).astype(jnp.bfloat16)
    arrived = jnp.concatenate(arrived, axis=1)
    before = jnp.sum((owner_of[None, :] < owner_of[:, None]).astype(jnp.int32), axis=1)
    position = jnp.arange(token_count, dtype=jnp.int32) - before
    grad_hidden = arrived.reshape(owner_count * capacity, hidden_width)[
        owner_of * capacity + position
    ]
    return (grad_a, grad_b, grad_hidden)


def solution(mesh):
    return jax.shard_map(
        shards,
        mesh=mesh,
        in_specs=(
            P("dp", "fsdp"),
            P("dp", "fsdp"),
            P("dp"),
            P("dp", None, "fsdp"),
            P("dp", None, "fsdp"),
        ),
        out_specs=(P("dp", None, "fsdp"), P("dp", None, "fsdp"), P("dp", "fsdp")),
        check_vma=False,
    )
```

time: 384 us -> 511 us (1.33)
  local copies, waits for them, and re-layouts: 23.7 us -> 57.6 us
  waiting for transfers between devices: 278 us -> 308 us
  blocking collectives: 25 us -> 48.2 us
  starting transfers between devices: 17 us -> 34.2 us
  other arithmetic: 7.57 us -> 21.2 us
  matrix products: 25.3 us -> 32.7 us
    all_to_all x1 -> x2, waiting for transfers between devices: 114 us -> 148 us  [shards(): lax.all_to_all(returned, 'dp', split_axis=0, concat_axis=0, tiled=True)]
    reshape x0 -> x4, local copies, waits for them, and re-layouts: none -> 24.3 us  [the longest x2 13.7 us: shards(): recv = recv.reshape(rows, hidden_width + model_width + id_width)]
    psum x1 -> x2, blocking collectives: 25 us -> 48.2 us  [shards(): full = lax.psum(jnp.concatenate([pick_down, pick_back], axis=1), 'fsdp')]
    select_n x2 -> x5, other arithmetic: 0.09 us -> 10.5 us  [the longest x3 10.5 us: shards(): table.at[row_index[:, k * piece:(k + 1) * piece]]]
    all_to_all x1 -> x2, starting transfers between devices: 9.9 us -> 18.8 us  [shards(): recv = lax.all_to_all(send, 'dp', split_axis=0, concat_axis=0, tiled=True)]
    gather x5, local copies, waits for them, and re-layouts: 22.1 us -> 30.7 us  [the longest x4 22.7 us: shards(): table.at[row_index[:, k * piece:(k + 1) * piece]]]
    all_to_all x1 -> x2, starting transfers between devices: 7.06 us -> 15.4 us  [shards(): lax.all_to_all(returned, 'dp', split_axis=0, concat_axis=0, tiled=True)]
    dot_general x2 -> x4, matrix products: 8.05 us -> 12.6 us  [contract_cols(): lax.dot_general(left, right, (((1,), (1,)), ((), ())), preferred_element_...]
  transfers between devices with their start and end apart: 2 -> 4, of which waited for: 2 -> 4; matrix products, arithmetic and copies ran while one was open for 3% -> 10% of each run, Pallas kernels for 0% -> 0%
where the time goes in v2:
time: 511 us; the launch traced here: 503 us
  waiting for transfers between devices  308 us (60%)
  local copies, waits for them, and re-layouts  57.6 us (11%)
  blocking collectives  48.2 us (9%)
  starting transfers between devices  34.2 us (7%)
  matrix products  32.7 us (6%)
  other arithmetic  21.2 us (4%)
    all_to_all x2, waiting for transfers between devices, shards(): recv = lax.all_to_all(send, 'dp', split_axis=0, concat_axis=0, tiled=True)  161 us
    all_to_all x2, waiting for transfers between devices, shards(): lax.all_to_all(returned, 'dp', split_axis=0, concat_axis=0, tiled=True)  148 us
    psum x2, blocking collectives, shards(): full = lax.psum(jnp.concatenate([pick_down, pick_back], axis=1), 'fsdp')  48.2 us
    gather x4, local copies, waits for them, and re-layouts, shards(): table.at[row_index[:, k * piece:(k + 1) * piece]]  22.7 us
    all_to_all x2, starting transfers between devices, shards(): recv = lax.all_to_all(send, 'dp', split_axis=0, concat_axis=0, tiled=True)  18.8 us
    all_to_all x2, starting transfers between devices, shards(): lax.all_to_all(returned, 'dp', split_axis=0, concat_axis=0, tiled=True)  15.4 us
    reshape x2, local copies, waits for them, and re-layouts, shards(): recv = recv.reshape(rows, hidden_width + model_width + id_width)  13.7 us
    dot_general x4, matrix products, contract_cols(): lax.dot_general(left, right, (((1,), (1,)), ((), ())), preferred_element_...  12.6 us
  transfers between devices with their start and end apart: 4, of which 4 were waited for; matrix products, arithmetic and copies ran while one was open for 10% of the time, Pallas kernels for 0%

profile of v2, /device:TPU:113, one launch (start us, length us, event | category | flops | bytes accessed | tf_op | source)
XLA Modules:
  0.0 503.0 jit_solution(9303705913638020247)
XLA Ops:
  8.7 6.8 %reshape.229 = bf16[32,12,4736]{2,1,0:T(8,128)(2,1)} reshape(bf16[384,4736]{1,0:T(8,128)(2,1)} %gather_fusion) | data formatting | bytes 7274496 | tf_op jit(solution)/shard_map/gather | solution.py:54
  15.5 5.2 %broadcast_select_fusion.1 = bf16[32,12,4736]{2,1,0:T(8,128)(2,1)} fusion(bf16[32,12,4736]{2,1,0:T(8,128)(2,1)} %reshape.229, pred[32,12]{1,0:T(8,128)(4,1)S(1)} %get-tuple-element.10), kind=kLoop, calls=%fused_computation.10 | loop fusion | flops 1818624 | bytes 7274880 | tf_op jit(solution)/shard_map/select_n | solution.py:54
  20.6 9.8 %all-to-all-start = ((bf16[32,12,4736]{2,1,0:T(8,128)(2,1)}), bf16[32,12,4736]{2,1,0:T(8,128)(2,1)}, u32[]{:S(2)}, u32[]{:S(2)}) async-start(bf16[32,12,4736]{2,1,0:T(8,128)(2,1)} %broadcast_select_fusion.1), calls=%async_computation | async-start | bytes 9699328 | tf_op jit(solution)/shard_map/all_to_all | solution.py:57
  30.5 4.6 gather_fusion.1
  35.1 6.8 %reshape.237 = bf16[32,12,4736]{2,1,0:T(8,128)(2,1)} reshape(bf16[384,4736]{1,0:T(8,128)(2,1)} %gather_fusion.1) | data formatting | bytes 7274496 | tf_op jit(solution)/shard_map/gather | solution.py:54
  41.9 5.2 %broadcast_select_fusion = bf16[32,12,4736]{2,1,0:T(8,128)(2,1)} fusion(bf16[32,12,4736]{2,1,0:T(8,128)(2,1)} %reshape.237, pred[32,12]{1,0:T(8,128)(4,1)S(1)} %get-tuple-element.9), kind=kLoop, calls=%fused_computation.9 | loop fusion | flops 1818624 | bytes 7274880 | tf_op jit(solution)/shard_map/select_n | solution.py:54
  47.1 91.4 %all-to-all-done = bf16[32,12,4736]{2,1,0:T(8,128)(2,1)} async-done(((bf16[32,12,4736]{2,1,0:T(8,128)(2,1)}), bf16[32,12,4736]{2,1,0:T(8,128)(2,1)}, u32[]{:S(2)}, u32[]{:S(2)}) %all-to-all-start) | async-done | bytes 3637280 | tf_op jit(solution)/shard_map/all_to_all | solution.py:57
  138.4 9.0 %all-to-all-start.1 = ((bf16[32,12,4736]{2,1,0:T(8,128)(2,1)}), bf16[32,12,4736]{2,1,0:T(8,128)(2,1)}, u32[]{:S(2)}, u32[]{:S(2)}) async-start(bf16[32,12,4736]{2,1,0:T(8,128)(2,1)} %broadcast_select_fusion), calls=%async_computation.1 | async-start | bytes 9699328 | tf_op jit(solution)/shard_map/all_to_all | solution.py:57
  147.5 6.9 %reshape.223 = bf16[384,4736]{1,0:T(8,128)(2,1)} reshape(bf16[32,12,4736]{2,1,0:T(8,128)(2,1)} %all-to-all-done) | data formatting | bytes 7274496 | tf_op jit(solution)/shard_map/reshape | solution.py:61
  161.4 24.6 %all-reduce.2 = bf16[384,128]{0,1:T(8,128)(2,1)S(1)} all-reduce(f32[384,128]{0,1:T(8,128)S(1)} %pad_maximum_fusion.2), channel_id=1, replica_groups=mesh['dp'=32,'fsdp'=8] {'fsdp'}, use_global_device_ids=true, to_apply=%region_4.5 | all-reduce | flops 49152 | bytes 294912 | tf_op jit(solution)/shard_map/psum | solution.py:70
  186.0 69.4 %all-to-all-done.1 = bf16[32,12,4736]{2,1,0:T(8,128)(2,1)} async-done(((bf16[32,12,4736]{2,1,0:T(8,128)(2,1)}), bf16[32,12,4736]{2,1,0:T(8,128)(2,1)}, u32[]{:S(2)}, u32[]{:S(2)}) %all-to-all-start.1) | async-done | bytes 3637280 | tf_op jit(solution)/shard_map/all_to_all | solution.py:57
  255.5 6.9 %reshape.224 = bf16[384,4736]{1,0:T(8,128)(2,1)} reshape(bf16[32,12,4736]{2,1,0:T(8,128)(2,1)} %all-to-all-done.1) | data formatting | bytes 7274496 | tf_op jit(solution)/shard_map/reshape | solution.py:61
  263.4 5.0 fusion.19
  270.3 23.5 %all-reduce.3 = bf16[384,128]{0,1:T(8,128)(2,1)S(1)} all-reduce(f32[384,128]{0,1:T(8,128)S(1)} %pad_maximum_fusion.3), channel_id=1, replica_groups=mesh['dp'=32,'fsdp'=8] {'fsdp'}, use_global_device_ids=true, to_apply=%region_7.8 | all-reduce | flops 49152 | bytes 294912 | tf_op jit(solution)/shard_map/psum | solution.py:70
  293.8 5.2 %fusion.1 = bf16[384,3584]{1,0:T(8,128)(2,1)} fusion(bf16[8,64,3584]{2,1,0:T(8,128)(2,1)} %param.8, bf16[384,64]{0,1:T(8,128)(2,1)S(1)} %get-tuple-element.6, bf16[384,8]{0,1:T(8,128)(2,1)S(1)} %get-tuple-element.17), kind=kOutput, calls=%fused_computation.7 | convolution fusion | flops 1410859008 | bytes 6477824 | tf_op jit(solution)/shard_map/dot_general | solution.py:76
  299.0 5.3 %reshape.226 = bf16[32,12,3584]{2,1,0:T(8,128)(2,1)} reshape(bf16[384,3584]{1,0:T(8,128)(2,1)} %fusion.1) | data formatting | bytes 5505024 | tf_op jit(solution)/shard_map/reshape | solution.py:79
  304.3 8.6 %all-to-all-start.3 = ((bf16[32,12,3584]{2,1,0:T(8,128)(2,1)}), bf16[32,12,3584]{2,1,0:T(8,128)(2,1)}, u32[]{:S(2)}, u32[]{:S(2)}) async-start(bf16[32,12,3584]{2,1,0:T(8,128)(2,1)} %reshape.226), calls=%async_computation.3 | async-start | bytes 7340032 | tf_op jit(solution)/shard_map/all_to_all | solution.py:80
  312.9 5.2 %fusion = bf16[384,3584]{1,0:T(8,128)(2,1)} fusion(bf16[8,64,3584]{2,1,0:T(8,128)(2,1)} %param.8, bf16[384,64]{0,1:T(8,128)(2,1)S(1)} %get-tuple-element.8, bf16[384,8]{0,1:T(8,128)(2,1)S(1)} %get-tuple-element.19), kind=kOutput, calls=%fused_computation.6 | convolution fusion | flops 1410859008 | bytes 6477824 | tf_op jit(solution)/shard_map/dot_general | solution.py:76
  318.1 5.3 %reshape.225 = bf16[32,12,3584]{2,1,0:T(8,128)(2,1)} reshape(bf16[384,3584]{1,0:T(8,128)(2,1)} %fusion) | data formatting | bytes 5505024 | tf_op jit(solution)/shard_map/reshape | solution.py:79
  323.4 73.9 %all-to-all-done.3 = bf16[32,12,3584]{2,1,0:T(8,128)(2,1)} async-done(((bf16[32,12,3584]{2,1,0:T(8,128)(2,1)}), bf16[32,12,3584]{2,1,0:T(8,128)(2,1)}, u32[]{:S(2)}, u32[]{:S(2)}) %all-to-all-start.3) | async-done | bytes 2752544 | tf_op jit(solution)/shard_map/all_to_all | solution.py:80
  397.3 6.9 %all-to-all-start.2 = ((bf16[32,12,3584]{2,1,0:T(8,128)(2,1)}), bf16[32,12,3584]{2,1,0:T(8,128)(2,1)}, u32[]{:S(2)}, u32[]{:S(2)}) async-start(bf16[32,12,3584]{2,1,0:T(8,128)(2,1)} %reshape.225), calls=%async_computation.2 | async-start | bytes 7340032 | tf_op jit(solution)/shard_map/all_to_all | solution.py:80
  414.3 73.6 %all-to-all-done.2 = bf16[32,12,3584]{2,1,0:T(8,128)(2,1)} async-done(((bf16[32,12,3584]{2,1,0:T(8,128)(2,1)}), bf16[32,12,3584]{2,1,0:T(8,128)(2,1)}, u32[]{:S(2)}, u32[]{:S(2)}) %all-to-all-start.2) | async-done | bytes 2752544 | tf_op jit(solution)/shard_map/all_to_all | solution.py:80
  487.9 7.1 %pad_maximum_fusion = bf16[32,24,3584]{2,1,0:T(8,128)(2,1)} fusion(bf16[32,12,3584]{2,1,0:T(8,128)(2,1)} %all-to-all-done.3, bf16[32,12,3584]{2,1,0:T(8,128)(2,1)} %all-to-all-done.2), kind=kLoop, calls=%fused_computation.8 | loop fusion | flops 11010048 | bytes 11010048 | tf_op jit(solution)/shard_map/concatenate | solution.py:87
  495.0 8.0 %gather_fusion.2 = bf16[256,3584]{1,0:T(8,128)(2,1)} fusion(bf16[768,3584]{1,0:T(8,128)(2,1)} %bitcast.46, s32[1024]{0:T(1024)S(1)} %pad_clamp_fusion), kind=kCustom, calls=%fused_computation.2 | custom fusion | bytes 3671040 | tf_op jit(solution)/shard_map/gather | solution.py:90
  (45 shorter events, 28.2 us)
Async XLA Ops:
  0.6 154.9 %copy-start = (bf16[8,64,1024]{2,1,0:T(8,128)(2,1)S(1)}, bf16[8,64,1024]{2,1,0:T(8,128)(2,1)}, u32[]{:S(2)}) copy-start(bf16[8,64,1024]{2,1,0:T(8,128)(2,1)} %param.9) | copy-start | bytes 3145732
  20.6 117.8 %all-to-all-start = ((bf16[32,12,4736]{2,1,0:T(8,128)(2,1)}), bf16[32,12,4736]{2,1,0:T(8,128)(2,1)}, u32[]{:S(2)}, u32[]{:S(2)}) async-start(bf16[32,12,4736]{2,1,0:T(8,128)(2,1)} %broadcast_select_fusion.1), calls=%async_computation | async-start | bytes 9699328 | tf_op jit(solution)/shard_map/all_to_all | solution.py:57
  138.4 117.0 %all-to-all-start.1 = ((bf16[32,12,4736]{2,1,0:T(8,128)(2,1)}), bf16[32,12,4736]{2,1,0:T(8,128)(2,1)}, u32[]{:S(2)}, u32[]{:S(2)}) async-start(bf16[32,12,4736]{2,1,0:T(8,128)(2,1)} %broadcast_select_fusion), calls=%async_computation.1 | async-start | bytes 9699328 | tf_op jit(solution)/shard_map/all_to_all | solution.py:57
  154.3 3.1 copy-start.1
  304.3 93.0 %all-to-all-start.3 = ((bf16[32,12,3584]{2,1,0:T(8,128)(2,1)}), bf16[32,12,3584]{2,1,0:T(8,128)(2,1)}, u32[]{:S(2)}, u32[]{:S(2)}) async-start(bf16[32,12,3584]{2,1,0:T(8,128)(2,1)} %reshape.226), calls=%async_computation.3 | async-start | bytes 7340032 | tf_op jit(solution)/shard_map/all_to_all | solution.py:80
  397.3 90.6 %all-to-all-start.2 = ((bf16[32,12,3584]{2,1,0:T(8,128)(2,1)}), bf16[32,12,3584]{2,1,0:T(8,128)(2,1)}, u32[]{:S(2)}, u32[]{:S(2)}) async-start(bf16[32,12,3584]{2,1,0:T(8,128)(2,1)} %reshape.225), calls=%async_computation.2 | async-start | bytes 7340032 | tf_op jit(solution)/shard_map/all_to_all | solution.py:80
  404.2 2.5 copy-start.3
  404.5 3.8 copy-start.2

commit v3 on v1

--- a/solution.py
+++ b/solution.py
@@ -30,25 +30,29 @@
     starts = jnp.cumsum(counts) - counts
     slot_index = jnp.arange(capacity, dtype=jnp.int32)
     usable = slot_index[None, :] < counts[:, None]
-    row_index = jnp.where(usable, starts[:, None] + slot_index[None, :], 0)
+    total_rows = owner_count * capacity
+    token_index = jnp.arange(token_count, dtype=jnp.int32)
+    wanted = jnp.where(usable, starts[:, None] + slot_index[None, :], -1).reshape(total_rows)
+    pick = (wanted[:, None] == token_index[None, :]).astype(jnp.bfloat16)
     id_width = 128
-    send_local = jnp.where(usable, region_ids[row_index] % local_count, local_count).astype(
-        jnp.bfloat16
-    )
-    send = jnp.concatenate(
+    table = jnp.concatenate(
         [
-            hidden[row_index],
-            cotangent[row_index],
-            jnp.broadcast_to(send_local[:, :, None], (owner_count, capacity, id_width)),
+            hidden,
+            cotangent,
+            jnp.broadcast_to(
+                (region_ids % local_count + 1).astype(jnp.bfloat16)[:, None],
+                (token_count, id_width),
+            ),
         ],
         axis=-1,
     )
+    send = jnp.dot(pick, table, preferred_element_type=jnp.float32).astype(jnp.bfloat16)
+    send = send.reshape(owner_count, capacity, hidden_width + model_width + id_width)
     recv = lax.all_to_all(send, "dp", split_axis=0, concat_axis=0, tiled=True)
-    total_rows = owner_count * capacity
     recv = recv.reshape(total_rows, hidden_width + model_width + id_width)
     got_hidden = recv[:, :hidden_width]
     got_cotangent = recv[:, hidden_width : hidden_width + model_width]
-    got_local = recv[:, hidden_width + model_width]
+    got_local = recv[:, hidden_width + model_width] - 1
     local_ids = jnp.arange(local_count).astype(jnp.bfloat16)
     onehot = (got_local[:, None] == local_ids[None, :]).astype(jnp.float32)
     flat_a = adapter_a.reshape(local_count * rank_width, hidden_width)
@@ -77,8 +81,12 @@
     returned = returned.reshape(owner_count, capacity, hidden_width)
     arrived = lax.all_to_all(returned, "dp", split_axis=0, concat_axis=0, tiled=True)
     before = jnp.sum((owner_of[None, :] < owner_of[:, None]).astype(jnp.int32), axis=1)
-    position = jnp.arange(token_count, dtype=jnp.int32) - before
-    grad_hidden = arrived.reshape(total_rows, hidden_width)[owner_of * capacity + position]
+    source = owner_of * capacity + token_index - before
+    slot_all = jnp.arange(total_rows, dtype=jnp.int32)
+    place = (source[:, None] == slot_all[None, :]).astype(jnp.bfloat16)
+    grad_hidden = jnp.dot(
+        place, arrived.reshape(total_rows, hidden_width), preferred_element_type=jnp.float32
+    ).astype(jnp.bfloat16)
     return (grad_a, grad_b, grad_hidden)
 
 

time: 384 us -> 370 us (0.964)
  local copies, waits for them, and re-layouts: 23.7 us -> 0.3 us
  matrix products: 25.3 us -> 38.6 us
  other arithmetic: 7.57 us -> 2.54 us
    gather x5 -> x0, local copies, waits for them, and re-layouts: 22.1 us -> none  [the longest x1 8.03 us: shards(): arrived.reshape(total_rows, hidden_width)[owner_of * capacity + position]]
    dot_general x0 -> x2, matrix products: none -> 12.2 us  [the longest x1 6.82 us: shards(): jnp.dot(pick, table, preferred_element_type=jnp.float32)]
    concatenate x1 -> x0, other arithmetic: 5.99 us -> none  [shards(): jnp.concatenate([hidden[row_index], cotangent[row_index], jnp.broadcast_t...]
where the time goes in v3:
time: 370 us; the launch traced here: 363 us
  waiting for transfers between devices  278 us (75%)
  matrix products  38.6 us (10%)
  blocking collectives  25 us (7%)
  starting transfers between devices  17 us (5%)
    all_to_all x1, waiting for transfers between devices, shards(): recv = lax.all_to_all(send, 'dp', split_axis=0, concat_axis=0, tiled=True)  163 us
    all_to_all x1, waiting for transfers between devices, shards(): lax.all_to_all(returned, 'dp', split_axis=0, concat_axis=0, tiled=True)  115 us
    psum x1, blocking collectives, shards(): full = lax.psum(jnp.concatenate([pick_down, pick_back], axis=1), 'fsdp')  25 us
    dot_general x2, matrix products, contract_rows(): lax.dot_general(left, right, (((0,), (0,)), ((), ())), preferred_element_...  10.4 us
    all_to_all x1, starting transfers between devices, shards(): recv = lax.all_to_all(send, 'dp', split_axis=0, concat_axis=0, tiled=True)  9.77 us
    dot_general x2, matrix products, contract_cols(): lax.dot_general(left, right, (((1,), (1,)), ((), ())), preferred_element_...  9.16 us
  transfers between devices with their start and end apart: 2, of which 2 were waited for; matrix products, arithmetic and copies ran while one was open for 3% of the time, Pallas kernels for 0%

profile of v3, /device:TPU:113, one launch (start us, length us, event | category | flops | bytes accessed | tf_op | source)
XLA Modules:
  0.0 362.5 jit_solution(12109619107542652340)
XLA Ops:
  0.6 0.0 copy-start
  0.6 0.8 and_select_fusion.1
  1.4 0.1 convert_reduce_fusion.1
  1.5 0.1 copy.10
  1.6 0.1 reduce-window.8
  1.7 0.1 reduce
  1.8 0.1 add_select_fusion
  1.9 0.1 select_n.25
  2.0 0.1 broadcast_in_dim.6
  2.1 6.8 %convolution_convert_fusion = bf16[768,4736]{1,0:T(8,128)(2,1)} fusion(bf16[256,128]{1,0:T(8,128)(2,1)S(1)} %broadcast_in_dim.6, bf16[256,1024]{1,0:T(8,128)(2,1)} %param.6, bf16[256,3584]{1,0:T(8,128)(2,1)} %param.5, s32[768]{0:T(1024)S(1)} %select_n.25), kind=kOutput, calls=%fused_computation.1 | convolution fusion | flops 1873379328 | bytes 9702400 | tf_op jit(solution)/shard_map/dot_general | solution.py:49
  8.9 9.8 %all-to-all-start = ((bf16[32,24,4736]{2,1,0:T(8,128)(2,1)}), bf16[32,24,4736]{2,1,0:T(8,128)(2,1)}, u32[]{:S(2)}, u32[]{:S(2)}) async-start(bf16[32,24,4736]{2,1,0:T(8,128)(2,1)} %bitcast.35), calls=%async_computation | async-start | bytes 14548992 | tf_op jit(solution)/shard_map/all_to_all | solution.py:51
  18.7 162.9 %all-to-all-done = bf16[32,24,4736]{2,1,0:T(8,128)(2,1)} async-done(((bf16[32,24,4736]{2,1,0:T(8,128)(2,1)}), bf16[32,24,4736]{2,1,0:T(8,128)(2,1)}, u32[]{:S(2)}, u32[]{:S(2)}) %all-to-all-start) | async-done | bytes 7274528 | tf_op jit(solution)/shard_map/all_to_all | solution.py:51
  181.6 1.1 fusion.17
  182.7 0.1 fusion.18
  182.8 6.7 %multiply_reduce_fusion.1 = f32[768,64]{0,1:T(8,128)S(1)} fusion(bf16[8,64,3584]{2,1,0:T(8,128)(2,1)} %param.8, bf16[768,4736]{1,0:T(8,128)(2,1)} %bitcast.2, f32[768,8]{0,1:T(8,128)S(1)} %get-tuple-element.6), kind=kOutput, calls=%fused_computation.13 | convolution fusion | flops 2819309568 | bytes 9396224 | tf_op jit(solution)/shard_map/dot_general | solution.py:14
  189.5 2.4 multiply_reduce_fusion
  192.0 25.0 %all-reduce.1 = bf16[768,128]{0,1:T(8,128)(2,1)S(1)} all-reduce(f32[768,128]{0,1:T(8,128)S(1)} %pad_maximum_fusion), channel_id=1, replica_groups=mesh['dp'=32,'fsdp'=8] {'fsdp'}, use_global_device_ids=true, to_apply=%region_4.5 | all-reduce | flops 98304 | bytes 589824 | tf_op jit(solution)/shard_map/psum | solution.py:64
  217.0 6.9 %bitcast_convert_fusion = bf16[768,3584]{1,0:T(8,128)(2,1)} fusion(bf16[8,64,3584]{2,1,0:T(8,128)(2,1)} %param.8, bf16[768,64]{0,1:T(8,128)(2,1)S(1)} %get-tuple-element.4, bf16[768,8]{0,1:T(8,128)(2,1)S(1)} %get-tuple-element.5), kind=kOutput, calls=%fused_computation | convolution fusion | flops 2821718016 | bytes 9285632 | tf_op jit(solution)/shard_map/dot_general | solution.py:80
  223.9 7.3 %all-to-all-start.1 = ((bf16[32,24,3584]{2,1,0:T(8,128)(2,1)}), bf16[32,24,3584]{2,1,0:T(8,128)(2,1)}, u32[]{:S(2)}, u32[]{:S(2)}) async-start(bf16[32,24,3584]{2,1,0:T(8,128)(2,1)} %bitcast.36), calls=%async_computation.1 | async-start | bytes 11010048 | tf_op jit(solution)/shard_map/all_to_all | solution.py:82
  231.2 0.2 convert_reduce_fusion
  231.3 3.4 convolution_convert_fusion.3
  234.7 7.0 %convolution_convert_fusion.1 = bf16[8,64,3584]{2,1,0:T(8,128)(2,1)} fusion(bf16[768,4736]{1,0:T(8,128)(2,1)} %bitcast.2, bf16[768,64]{0,1:T(8,128)(2,1)S(1)} %get-tuple-element.4, bf16[768,8]{0,1:T(8,128)(2,1)S(1)} %get-tuple-element.5), kind=kOutput, calls=%fused_computation.2 | convolution fusion | flops 2820800512 | bytes 9285632 | tf_op jit(solution)/shard_map/dot_general | solution.py:8
  241.7 115.4 %all-to-all-done.1 = bf16[32,24,3584]{2,1,0:T(8,128)(2,1)} async-done(((bf16[32,24,3584]{2,1,0:T(8,128)(2,1)}), bf16[32,24,3584]{2,1,0:T(8,128)(2,1)}, u32[]{:S(2)}, u32[]{:S(2)}) %all-to-all-start.1) | async-done | bytes 5505056 | tf_op jit(solution)/shard_map/all_to_all | solution.py:82
  357.1 5.4 %convolution_convert_fusion.2 = bf16[256,3584]{1,0:T(8,128)(2,1)} fusion(bf16[768,3584]{1,0:T(8,128)(2,1)} %bitcast.13, s32[256]{0:T(256)S(1)} %add_subtract_fusion), kind=kOutput, calls=%fused_computation.4 | convolution fusion | flops 1410400256 | bytes 7341056 | tf_op jit(solution)/shard_map/dot_general | solution.py:87
  (6 shorter events, 0.1 us)
Async XLA Ops:
  0.6 188.9 %copy-start = (bf16[8,64,1024]{2,1,0:T(8,128)(2,1)S(1)}, bf16[8,64,1024]{2,1,0:T(8,128)(2,1)}, u32[]{:S(2)}) copy-start(bf16[8,64,1024]{2,1,0:T(8,128)(2,1)} %param.9) | copy-start | bytes 3145732
  8.9 172.7 %all-to-all-start = ((bf16[32,24,4736]{2,1,0:T(8,128)(2,1)}), bf16[32,24,4736]{2,1,0:T(8,128)(2,1)}, u32[]{:S(2)}, u32[]{:S(2)}) async-start(bf16[32,24,4736]{2,1,0:T(8,128)(2,1)} %bitcast.35), calls=%async_computation | async-start | bytes 14548992 | tf_op jit(solution)/shard_map/all_to_all | solution.py:51
  223.9 133.2 %all-to-all-start.1 = ((bf16[32,24,3584]{2,1,0:T(8,128)(2,1)}), bf16[32,24,3584]{2,1,0:T(8,128)(2,1)}, u32[]{:S(2)}, u32[]{:S(2)}) async-start(bf16[32,24,3584]{2,1,0:T(8,128)(2,1)} %bitcast.36), calls=%async_computation.1 | async-start | bytes 11010048 | tf_op jit(solution)/shard_map/all_to_all | solution.py:82

commit v4 on v3

--- a/solution.py
+++ b/solution.py
@@ -14,6 +14,17 @@
     return lax.dot_general(
         left, right, (((1,), (1,)), ((), ())), preferred_element_type=jnp.float32
     )
+
+
+def fsdp_sum(x):
+    n = lax.axis_size("fsdp")
+    if n & (n - 1):
+        return lax.psum(x, "fsdp")
+    step = 1
+    while step < n:
+        x = x + lax.ppermute(x, "fsdp", [(i, i ^ step) for i in range(n)])
+        step *= 2
+    return x
 
 
 def shards(hidden, cotangent, region_ids, adapter_a, adapter_b):
@@ -34,26 +45,23 @@
     token_index = jnp.arange(token_count, dtype=jnp.int32)
     wanted = jnp.where(usable, starts[:, None] + slot_index[None, :], -1).reshape(total_rows)
     pick = (wanted[:, None] == token_index[None, :]).astype(jnp.bfloat16)
-    id_width = 128
-    table = jnp.concatenate(
-        [
-            hidden,
-            cotangent,
-            jnp.broadcast_to(
-                (region_ids % local_count + 1).astype(jnp.bfloat16)[:, None],
-                (token_count, id_width),
-            ),
-        ],
-        axis=-1,
-    )
+    table = jnp.concatenate([hidden, cotangent], axis=-1)
     send = jnp.dot(pick, table, preferred_element_type=jnp.float32).astype(jnp.bfloat16)
-    send = send.reshape(owner_count, capacity, hidden_width + model_width + id_width)
+    send = send.reshape(owner_count, capacity, hidden_width + model_width)
     recv = lax.all_to_all(send, "dp", split_axis=0, concat_axis=0, tiled=True)
-    recv = recv.reshape(total_rows, hidden_width + model_width + id_width)
+    recv = recv.reshape(total_rows, hidden_width + model_width)
     got_hidden = recv[:, :hidden_width]
-    got_cotangent = recv[:, hidden_width : hidden_width + model_width]
-    got_local = recv[:, hidden_width + model_width] - 1
-    local_ids = jnp.arange(local_count).astype(jnp.bfloat16)
+    got_cotangent = recv[:, hidden_width:]
+    me = lax.axis_index("dp")
+    all_ids = lax.all_gather(region_ids, "dp")
+    all_owner = all_ids // local_count
+    in_counts = jnp.sum((all_owner == me).astype(jnp.int32), axis=1)
+    in_starts = jnp.sum((all_owner < me).astype(jnp.int32), axis=1)
+    hit = token_index[None, None, :] == (in_starts[:, None] + slot_index[None, :])[:, :, None]
+    slot_region = jnp.sum(jnp.where(hit, all_ids[:, None, :] % local_count, 0), axis=2)
+    valid = slot_index[None, :] < in_counts[:, None]
+    got_local = jnp.where(valid, slot_region, -1).reshape(total_rows)
+    local_ids = jnp.arange(local_count, dtype=jnp.int32)
     onehot = (got_local[:, None] == local_ids[None, :]).astype(jnp.float32)
     flat_a = adapter_a.reshape(local_count * rank_width, hidden_width)
     flat_b = adapter_b.reshape(local_count * rank_width, model_width)
@@ -61,7 +69,7 @@
     part_back = contract_cols(got_cotangent, flat_b).reshape(total_rows, local_count, rank_width)
     pick_down = jnp.sum(part_down * onehot[:, :, None], axis=1)
     pick_back = jnp.sum(part_back * onehot[:, :, None], axis=1)
-    full = lax.psum(jnp.concatenate([pick_down, pick_back], axis=1), "fsdp")
+    full = fsdp_sum(jnp.concatenate([pick_down, pick_back], axis=1))
     full_down = full[:, :rank_width].astype(jnp.bfloat16)
     full_back = full[:, rank_width:].astype(jnp.bfloat16)
     mask = onehot.astype(jnp.bfloat16)[:, :, None]

time: 370 us -> 386 us (1.043)
  blocking collectives: 25 us -> 182 us
  waiting for transfers between devices: 278 us -> 132 us
  starting transfers between devices: 17 us -> 28 us
    all_gather x0 -> x1, blocking collectives: none -> 182 us  [shards(): all_ids = lax.all_gather(region_ids, 'dp')]
    all_to_all x1, waiting for transfers between devices: 163 us -> 0.01 us  [shards(): recv = lax.all_to_all(send, 'dp', split_axis=0, concat_axis=0, tiled=True)]
    psum x1 -> x0, blocking collectives: 25 us -> none  [shards(): full = lax.psum(jnp.concatenate([pick_down, pick_back], axis=1), 'fsdp')]
    ppermute x0 -> x3, waiting for transfers between devices: none -> 21.6 us  [fsdp_sum(): x = x + lax.ppermute(x, 'fsdp', [(i, i ^ step) for i in range(n)])]
    ppermute x0 -> x3, starting transfers between devices: none -> 9.76 us  [fsdp_sum(): x = x + lax.ppermute(x, 'fsdp', [(i, i ^ step) for i in range(n)])]
    all_to_all x1, waiting for transfers between devices: 115 us -> 111 us  [shards(): lax.all_to_all(returned, 'dp', split_axis=0, concat_axis=0, tiled=True)]
  transfers between devices with their start and end apart: 2 -> 5, of which waited for: 2 -> 4; matrix products, arithmetic and copies ran while one was open for 3% -> 3% of each run, Pallas kernels for 0% -> 0%
where the time goes in v4:
time: 386 us; the launch traced here: 382 us
  blocking collectives  182 us (47%)
  waiting for transfers between devices  132 us (34%)
  matrix products  35.6 us (9%)
  starting transfers between devices  28 us (7%)
    all_gather x1, blocking collectives, shards(): all_ids = lax.all_gather(region_ids, 'dp')  182 us
    all_to_all x1, waiting for transfers between devices, shards(): lax.all_to_all(returned, 'dp', split_axis=0, concat_axis=0, tiled=True)  111 us
    ppermute x3, waiting for transfers between devices, fsdp_sum(): x = x + lax.ppermute(x, 'fsdp', [(i, i ^ step) for i in range(n)])  21.6 us
    dot_general x2, matrix products, contract_rows(): lax.dot_general(left, right, (((0,), (0,)), ((), ())), preferred_element_...  10.3 us
    all_to_all x1, starting transfers between devices, shards(): recv = lax.all_to_all(send, 'dp', split_axis=0, concat_axis=0, tiled=True)  9.9 us
    ppermute x3, starting transfers between devices, fsdp_sum(): x = x + lax.ppermute(x, 'fsdp', [(i, i ^ step) for i in range(n)])  9.76 us
    all_to_all x1, starting transfers between devices, shards(): lax.all_to_all(returned, 'dp', split_axis=0, concat_axis=0, tiled=True)  8.37 us
    dot_general x2, matrix products, contract_cols(): lax.dot_general(left, right, (((1,), (1,)), ((), ())), preferred_element_...  8.2 us
  transfers between devices with their start and end apart: 5, of which 4 were waited for; matrix products, arithmetic and copies ran while one was open for 3% of the time, Pallas kernels for 0%

profile of v4, /device:TPU:113, one launch (start us, length us, event | category | flops | bytes accessed | tf_op | source)
XLA Modules:
  0.0 381.8 jit_solution(8557456365355553909)
XLA Ops:
  0.6 0.8 and_select_fusion
  1.4 0.1 convert_reduce_fusion.1
  1.7 0.1 reduce
  1.9 0.1 select_n.50
  2.0 6.7 %convolution_convert_fusion = bf16[768,4608]{1,0:T(8,128)(2,1)} fusion(bf16[256,1024]{1,0:T(8,128)(2,1)} %param.6, bf16[256,3584]{1,0:T(8,128)(2,1)} %param.5, s32[768]{0:T(1024)S(1)} %select_n.50), kind=kOutput, calls=%fused_computation.1 | convolution fusion | flops 1820393472 | bytes 9440256 | tf_op jit(solution)/shard_map/dot_general | solution.py:49
  8.6 9.9 %all-to-all-start = ((bf16[32,24,4608]{2,1,0:T(8,128)(2,1)}), bf16[32,24,4608]{2,1,0:T(8,128)(2,1)}, u32[]{:S(2)}, u32[]{:S(2)}) async-start(bf16[32,24,4608]{2,1,0:T(8,128)(2,1)} %bitcast.62), calls=%async_computation | async-start | bytes 14155776 | tf_op jit(solution)/shard_map/all_to_all | solution.py:51
  18.6 182.1 %all-gather.1 = s32[32,1,256]{2,1,0:T(1,128)S(1)} all-gather(s32[1,1,256]{2,1,0:T(1,128)S(1)} %bitcast.64), channel_id=2, replica_groups=mesh['dp'=32,'fsdp'=8] {'dp'}, dimensions={0}, use_global_device_ids=true | all-gather | bytes 33792 | tf_op jit(solution)/shard_map/all_gather | solution.py:56
  200.7 0.1 convert_reduce_fusion.3
  200.9 0.8 select_reduce_fusion
  201.9 2.6 multiply_reduce_fusion
  204.5 5.6 %multiply_reduce_fusion.1 = f32[768,64]{0,1:T(8,128)S(1)} fusion(bf16[8,64,3584]{2,1,0:T(8,128)(2,1)S(1)} %copy-done.2, bf16[768,4608]{1,0:T(8,128)(2,1)} %bitcast.3, f32[768,8]{0,1:T(8,128)S(1)} %get-tuple-element.10), kind=kOutput, calls=%fused_computation.11 | convolution fusion | flops 2819309568 | bytes 9396224 | tf_op jit(solution)/shard_map/dot_general | solution.py:14
  210.1 8.6 %collective-permute-start = (f32[768,128]{0,1:T(8,128)S(1)}, f32[768,128]{0,1:T(8,128)S(1)}, u32[]{:S(2)}, u32[]{:S(2)}) collective-permute-start(f32[768,128]{0,1:T(8,128)S(1)} %pad_maximum_fusion), channel_id=1, source_target_pairs={{0,1},{1,0},{2,3},{3,2},{4,5},{5,4},{6,7},{7,6},{8,9},{9,8},{10,11... | collective-permute-start | bytes 1179656 | tf_op jit(solution)/shard_map/ppermute | solution.py:25
  218.7 1.3 collective-permute-done
  220.1 1.1 collective-permute-start.1
  221.2 9.3 %collective-permute-done.1 = f32[768,128]{0,1:T(8,128)S(1)} collective-permute-done((f32[768,128]{0,1:T(8,128)S(1)}, f32[768,128]{0,1:T(8,128)S(1)}, u32[]{:S(2)}, u32[]{:S(2)}) %collective-permute-start.1) | collective-permute-done | bytes 393248 | tf_op jit(solution)/shard_map/ppermute | solution.py:25
  230.6 0.1 collective-permute-start.2
  230.7 10.9 %collective-permute-done.2 = f32[768,128]{0,1:T(8,128)S(1)} collective-permute-done((f32[768,128]{0,1:T(8,128)S(1)}, f32[768,128]{0,1:T(8,128)S(1)}, u32[]{:S(2)}, u32[]{:S(2)}) %collective-permute-start.2) | collective-permute-done | bytes 393248 | tf_op jit(solution)/shard_map/ppermute | solution.py:25
  241.7 4.9 %bitcast_convert_fusion = bf16[768,3584]{1,0:T(8,128)(2,1)} fusion(bf16[8,64,3584]{2,1,0:T(8,128)(2,1)S(1)} %copy-done.2, bf16[768,64]{0,1:T(8,128)(2,1)S(1)} %get-tuple-element.6, bf16[768,8]{0,1:T(8,128)(2,1)S(1)} %get-tuple-element.9), kind=kOutput, calls=%fused_computation | convolution fusion | flops 2821718016 | bytes 9285632 | tf_op jit(solution)/shard_map/dot_general | solution.py:88
  246.6 8.4 %all-to-all-start.1 = ((bf16[32,24,3584]{2,1,0:T(8,128)(2,1)}), bf16[32,24,3584]{2,1,0:T(8,128)(2,1)}, u32[]{:S(2)}, u32[]{:S(2)}) async-start(bf16[32,24,3584]{2,1,0:T(8,128)(2,1)} %bitcast.63), calls=%async_computation.1 | async-start | bytes 11010048 | tf_op jit(solution)/shard_map/all_to_all | solution.py:90
  255.0 0.2 convert_reduce_fusion
  255.2 3.4 convolution_convert_fusion.3
  258.5 7.0 %convolution_convert_fusion.1 = bf16[8,64,3584]{2,1,0:T(8,128)(2,1)} fusion(bf16[768,4608]{1,0:T(8,128)(2,1)} %bitcast.3, bf16[768,64]{0,1:T(8,128)(2,1)S(1)} %get-tuple-element.6, bf16[768,8]{0,1:T(8,128)(2,1)S(1)} %get-tuple-element.9), kind=kOutput, calls=%fused_computation.2 | convolution fusion | flops 2820800512 | bytes 9285632 | tf_op jit(solution)/shard_map/dot_general | solution.py:8
  265.5 110.9 %all-to-all-done.1 = bf16[32,24,3584]{2,1,0:T(8,128)(2,1)} async-done(((bf16[32,24,3584]{2,1,0:T(8,128)(2,1)}), bf16[32,24,3584]{2,1,0:T(8,128)(2,1)}, u32[]{:S(2)}, u32[]{:S(2)}) %all-to-all-start.1) | async-done | bytes 5505056 | tf_op jit(solution)/shard_map/all_to_all | solution.py:90
  376.4 5.4 %convolution_convert_fusion.2 = bf16[256,3584]{1,0:T(8,128)(2,1)} fusion(bf16[768,3584]{1,0:T(8,128)(2,1)} %bitcast.14, s32[256]{0:T(256)S(1)} %add_subtract_fusion), kind=kOutput, calls=%fused_computation.4 | convolution fusion | flops 1410400256 | bytes 7341056 | tf_op jit(solution)/shard_map/dot_general | solution.py:95
  (22 shorter events, 0.7 us)
Async XLA Ops:
  0.6 201.2 %copy-start = (bf16[8,64,1024]{2,1,0:T(8,128)(2,1)S(1)}, bf16[8,64,1024]{2,1,0:T(8,128)(2,1)}, u32[]{:S(2)}) copy-start(bf16[8,64,1024]{2,1,0:T(8,128)(2,1)} %param.9) | copy-start | bytes 3145732
  8.6 9.9 %copy-start.1 = (s32[256]{0:T(256)S(1)}, s32[256]{0:T(256)}, u32[]{:S(2)}) copy-start(s32[256]{0:T(256)} %param.7) | copy-start | bytes 3076
  8.6 193.2 %all-to-all-start = ((bf16[32,24,4608]{2,1,0:T(8,128)(2,1)}), bf16[32,24,4608]{2,1,0:T(8,128)(2,1)}, u32[]{:S(2)}, u32[]{:S(2)}) async-start(bf16[32,24,4608]{2,1,0:T(8,128)(2,1)} %bitcast.62), calls=%async_computation | async-start | bytes 14155776 | tf_op jit(solution)/shard_map/all_to_all | solution.py:51
  201.9 2.6 copy-start.2
  210.1 9.9 %collective-permute-start = (f32[768,128]{0,1:T(8,128)S(1)}, f32[768,128]{0,1:T(8,128)S(1)}, u32[]{:S(2)}, u32[]{:S(2)}) collective-permute-start(f32[768,128]{0,1:T(8,128)S(1)} %pad_maximum_fusion), channel_id=1, source_target_pairs={{0,1},{1,0},{2,3},{3,2},{4,5},{5,4},{6,7},{7,6},{8,9},{9,8},{10,11... | collective-permute-start | bytes 1179656 | tf_op jit(solution)/shard_map/ppermute | solution.py:25
  220.1 10.4 %collective-permute-start.1 = (f32[768,128]{0,1:T(8,128)S(1)}, f32[768,128]{0,1:T(8,128)S(1)}, u32[]{:S(2)}, u32[]{:S(2)}) collective-permute-start(f32[768,128]{0,1:T(8,128)S(1)} %fusion.22), channel_id=1, source_target_pairs={{0,2},{1,3},{2,0},{3,1},{4,6},{5,7},{6,4},{7,5},{8,10},{9,11},{10,... | collective-permute-start | bytes 1179656 | tf_op jit(solution)/shard_map/ppermute | solution.py:25
  230.6 11.0 %collective-permute-start.2 = (f32[768,128]{0,1:T(8,128)S(1)}, f32[768,128]{0,1:T(8,128)S(1)}, u32[]{:S(2)}, u32[]{:S(2)}) collective-permute-start(f32[768,128]{0,1:T(8,128)S(1)} %add.58), channel_id=1, source_target_pairs={{0,4},{1,5},{2,6},{3,7},{4,0},{5,1},{6,2},{7,3},{8,12},{9,13},{10,... | collective-permute-start | bytes 1179656 | tf_op jit(solution)/shard_map/ppermute | solution.py:25
  246.6 129.8 %all-to-all-start.1 = ((bf16[32,24,3584]{2,1,0:T(8,128)(2,1)}), bf16[32,24,3584]{2,1,0:T(8,128)(2,1)}, u32[]{:S(2)}, u32[]{:S(2)}) async-start(bf16[32,24,3584]{2,1,0:T(8,128)(2,1)} %bitcast.63), calls=%async_computation.1 | async-start | bytes 11010048 | tf_op jit(solution)/shard_map/all_to_all | solution.py:90

commit v5 on v3

--- a/solution.py
+++ b/solution.py
@@ -14,6 +14,17 @@
     return lax.dot_general(
         left, right, (((1,), (1,)), ((), ())), preferred_element_type=jnp.float32
     )
+
+
+def fsdp_sum(x):
+    n = lax.axis_size("fsdp")
+    if n & (n - 1):
+        return lax.psum(x, "fsdp")
+    step = 1
+    while step < n:
+        x = x + lax.ppermute(x, "fsdp", [(i, i ^ step) for i in range(n)])
+        step *= 2
+    return x
 
 
 def shards(hidden, cotangent, region_ids, adapter_a, adapter_b):
@@ -61,7 +72,7 @@
     part_back = contract_cols(got_cotangent, flat_b).reshape(total_rows, local_count, rank_width)
     pick_down = jnp.sum(part_down * onehot[:, :, None], axis=1)
     pick_back = jnp.sum(part_back * onehot[:, :, None], axis=1)
-    full = lax.psum(jnp.concatenate([pick_down, pick_back], axis=1), "fsdp")
+    full = fsdp_sum(jnp.concatenate([pick_down, pick_back], axis=1))
     full_down = full[:, :rank_width].astype(jnp.bfloat16)
     full_back = full[:, rank_width:].astype(jnp.bfloat16)
     mask = onehot.astype(jnp.bfloat16)[:, :, None]

time: 370 us -> 359 us (0.970); the launches traced: 363 us -> 355 us
  blocking collectives: 25 us -> 0 us
  waiting for transfers between devices: 278 us -> 295 us
    psum x1 -> x0, blocking collectives: 25 us -> none  [shards(): full = lax.psum(jnp.concatenate([pick_down, pick_back], axis=1), 'fsdp')]
    ppermute x0 -> x3, waiting for transfers between devices: none -> 21.5 us  [fsdp_sum(): x = x + lax.ppermute(x, 'fsdp', [(i, i ^ step) for i in range(n)])]
    all_to_all x1, waiting for transfers between devices: 115 us -> 111 us  [shards(): lax.all_to_all(returned, 'dp', split_axis=0, concat_axis=0, tiled=True)]
  transfers between devices with their start and end apart: 2 -> 5, of which waited for: 2 -> 5; matrix products, arithmetic and copies ran while one was open for 3% -> 3% of each run, Pallas kernels for 0% -> 0%
where the time goes in v5:
time: 359 us; the launch traced here: 355 us
  waiting for transfers between devices  295 us (82%)
  matrix products  36.7 us (10%)
  starting transfers between devices  19.4 us (5%)
    all_to_all x1, waiting for transfers between devices, shards(): recv = lax.all_to_all(send, 'dp', split_axis=0, concat_axis=0, tiled=True)  163 us
    all_to_all x1, waiting for transfers between devices, shards(): lax.all_to_all(returned, 'dp', split_axis=0, concat_axis=0, tiled=True)  111 us
    ppermute x3, waiting for transfers between devices, fsdp_sum(): x = x + lax.ppermute(x, 'fsdp', [(i, i ^ step) for i in range(n)])  21.5 us
    dot_general x2, matrix products, contract_rows(): lax.dot_general(left, right, (((0,), (0,)), ((), ())), preferred_element_...  10.4 us
    all_to_all x1, starting transfers between devices, shards(): recv = lax.all_to_all(send, 'dp', split_axis=0, concat_axis=0, tiled=True)  9.77 us
    dot_general x2, matrix products, contract_cols(): lax.dot_general(left, right, (((1,), (1,)), ((), ())), preferred_element_...  9.18 us
  transfers between devices with their start and end apart: 5, of which 5 were waited for; matrix products, arithmetic and copies ran while one was open for 3% of the time, Pallas kernels for 0%

profile of v5, /device:TPU:113, one launch (start us, length us, event | category | flops | bytes accessed | tf_op | source)
XLA Modules:
  0.0 355.3 jit_solution(15462828134588269793)
XLA Ops:
  0.6 0.8 and_select_fusion.1
  1.4 0.1 convert_reduce_fusion.1
  1.7 0.1 reduce
  1.9 0.1 select_n.25
  2.0 0.1 broadcast_in_dim.6
  2.1 6.8 %convolution_convert_fusion = bf16[768,4736]{1,0:T(8,128)(2,1)} fusion(bf16[256,128]{1,0:T(8,128)(2,1)S(1)} %broadcast_in_dim.6, bf16[256,1024]{1,0:T(8,128)(2,1)} %param.6, bf16[256,3584]{1,0:T(8,128)(2,1)} %param.5, s32[768]{0:T(1024)S(1)} %select_n.25), kind=kOutput, calls=%fused_computation.1 | convolution fusion | flops 1873379328 | bytes 9702400 | tf_op jit(solution)/shard_map/dot_general | solution.py:60
  8.9 9.8 %all-to-all-start = ((bf16[32,24,4736]{2,1,0:T(8,128)(2,1)}), bf16[32,24,4736]{2,1,0:T(8,128)(2,1)}, u32[]{:S(2)}, u32[]{:S(2)}) async-start(bf16[32,24,4736]{2,1,0:T(8,128)(2,1)} %bitcast.35), calls=%async_computation | async-start | bytes 14548992 | tf_op jit(solution)/shard_map/all_to_all | solution.py:62
  18.7 163.1 %all-to-all-done = bf16[32,24,4736]{2,1,0:T(8,128)(2,1)} async-done(((bf16[32,24,4736]{2,1,0:T(8,128)(2,1)}), bf16[32,24,4736]{2,1,0:T(8,128)(2,1)}, u32[]{:S(2)}, u32[]{:S(2)}) %all-to-all-start) | async-done | bytes 7274528 | tf_op jit(solution)/shard_map/all_to_all | solution.py:62
  181.8 1.1 fusion.17
  183.0 6.7 %multiply_reduce_fusion.1 = f32[768,64]{0,1:T(8,128)S(1)} fusion(bf16[8,64,3584]{2,1,0:T(8,128)(2,1)} %param.8, bf16[768,4736]{1,0:T(8,128)(2,1)} %bitcast.2, f32[768,8]{0,1:T(8,128)S(1)} %get-tuple-element.6), kind=kOutput, calls=%fused_computation.13 | convolution fusion | flops 2819309568 | bytes 9396224 | tf_op jit(solution)/shard_map/dot_general | solution.py:14
  189.7 2.4 multiply_reduce_fusion
  192.2 1.6 collective-permute-start
  193.9 1.3 collective-permute-done
  195.3 1.1 collective-permute-start.1
  196.4 9.3 %collective-permute-done.1 = f32[768,128]{0,1:T(8,128)S(1)} collective-permute-done((f32[768,128]{0,1:T(8,128)S(1)}, f32[768,128]{0,1:T(8,128)S(1)}, u32[]{:S(2)}, u32[]{:S(2)}) %collective-permute-start.1) | collective-permute-done | bytes 393248 | tf_op jit(solution)/shard_map/ppermute | solution.py:25
  205.7 0.1 collective-permute-start.2
  205.8 10.9 %collective-permute-done.2 = f32[768,128]{0,1:T(8,128)S(1)} collective-permute-done((f32[768,128]{0,1:T(8,128)S(1)}, f32[768,128]{0,1:T(8,128)S(1)}, u32[]{:S(2)}, u32[]{:S(2)}) %collective-permute-start.2) | collective-permute-done | bytes 393248 | tf_op jit(solution)/shard_map/ppermute | solution.py:25
  216.8 4.9 %bitcast_convert_fusion = bf16[768,3584]{1,0:T(8,128)(2,1)} fusion(bf16[8,64,3584]{2,1,0:T(8,128)(2,1)S(1)} %copy-done.1, bf16[768,64]{0,1:T(8,128)(2,1)S(1)} %get-tuple-element.4, bf16[768,8]{0,1:T(8,128)(2,1)S(1)} %get-tuple-element.5), kind=kOutput, calls=%fused_computation | convolution fusion | flops 2821718016 | bytes 9285632 | tf_op jit(solution)/shard_map/dot_general | solution.py:91
  221.7 6.8 %all-to-all-start.1 = ((bf16[32,24,3584]{2,1,0:T(8,128)(2,1)}), bf16[32,24,3584]{2,1,0:T(8,128)(2,1)}, u32[]{:S(2)}, u32[]{:S(2)}) async-start(bf16[32,24,3584]{2,1,0:T(8,128)(2,1)} %bitcast.36), calls=%async_computation.1 | async-start | bytes 11010048 | tf_op jit(solution)/shard_map/all_to_all | solution.py:93
  228.5 0.2 convert_reduce_fusion
  228.7 3.4 convolution_convert_fusion.3
  232.1 7.0 %convolution_convert_fusion.1 = bf16[8,64,3584]{2,1,0:T(8,128)(2,1)} fusion(bf16[768,4736]{1,0:T(8,128)(2,1)} %bitcast.2, bf16[768,64]{0,1:T(8,128)(2,1)S(1)} %get-tuple-element.4, bf16[768,8]{0,1:T(8,128)(2,1)S(1)} %get-tuple-element.5), kind=kOutput, calls=%fused_computation.2 | convolution fusion | flops 2820800512 | bytes 9285632 | tf_op jit(solution)/shard_map/dot_general | solution.py:8
  239.1 110.8 %all-to-all-done.1 = bf16[32,24,3584]{2,1,0:T(8,128)(2,1)} async-done(((bf16[32,24,3584]{2,1,0:T(8,128)(2,1)}), bf16[32,24,3584]{2,1,0:T(8,128)(2,1)}, u32[]{:S(2)}, u32[]{:S(2)}) %all-to-all-start.1) | async-done | bytes 5505056 | tf_op jit(solution)/shard_map/all_to_all | solution.py:93
  349.9 5.4 %convolution_convert_fusion.2 = bf16[256,3584]{1,0:T(8,128)(2,1)} fusion(bf16[768,3584]{1,0:T(8,128)(2,1)} %bitcast.13, s32[256]{0:T(256)S(1)} %add_subtract_fusion), kind=kOutput, calls=%fused_computation.4 | convolution fusion | flops 1410400256 | bytes 7341056 | tf_op jit(solution)/shard_map/dot_general | solution.py:98
  (16 shorter events, 0.5 us)
Async XLA Ops:
  0.6 189.1 %copy-start = (bf16[8,64,1024]{2,1,0:T(8,128)(2,1)S(1)}, bf16[8,64,1024]{2,1,0:T(8,128)(2,1)}, u32[]{:S(2)}) copy-start(bf16[8,64,1024]{2,1,0:T(8,128)(2,1)} %param.9) | copy-start | bytes 3145732
  8.9 172.9 %all-to-all-start = ((bf16[32,24,4736]{2,1,0:T(8,128)(2,1)}), bf16[32,24,4736]{2,1,0:T(8,128)(2,1)}, u32[]{:S(2)}, u32[]{:S(2)}) async-start(bf16[32,24,4736]{2,1,0:T(8,128)(2,1)} %bitcast.35), calls=%async_computation | async-start | bytes 14548992 | tf_op jit(solution)/shard_map/all_to_all | solution.py:62
  192.2 24.6 %copy-start.1 = (bf16[8,64,3584]{2,1,0:T(8,128)(2,1)S(1)}, bf16[8,64,3584]{2,1,0:T(8,128)(2,1)}, u32[]{:S(2)}) copy-start(bf16[8,64,3584]{2,1,0:T(8,128)(2,1)} %param.8) | copy-start | bytes 11010052
  192.2 3.0 collective-permute-start
  195.3 10.4 %collective-permute-start.1 = (f32[768,128]{0,1:T(8,128)S(1)}, f32[768,128]{0,1:T(8,128)S(1)}, u32[]{:S(2)}, u32[]{:S(2)}) collective-permute-start(f32[768,128]{0,1:T(8,128)S(1)} %fusion.22), channel_id=1, source_target_pairs={{0,2},{1,3},{2,0},{3,1},{4,6},{5,7},{6,4},{7,5},{8,10},{9,11},{10,... | collective-permute-start | bytes 1179656 | tf_op jit(solution)/shard_map/ppermute | solution.py:25
  205.7 11.0 %collective-permute-start.2 = (f32[768,128]{0,1:T(8,128)S(1)}, f32[768,128]{0,1:T(8,128)S(1)}, u32[]{:S(2)}, u32[]{:S(2)}) collective-permute-start(f32[768,128]{0,1:T(8,128)S(1)} %add.46), channel_id=1, source_target_pairs={{0,4},{1,5},{2,6},{3,7},{4,0},{5,1},{6,2},{7,3},{8,12},{9,13},{10,... | collective-permute-start | bytes 1179656 | tf_op jit(solution)/shard_map/ppermute | solution.py:25
  221.7 128.2 %all-to-all-start.1 = ((bf16[32,24,3584]{2,1,0:T(8,128)(2,1)}), bf16[32,24,3584]{2,1,0:T(8,128)(2,1)}, u32[]{:S(2)}, u32[]{:S(2)}) async-start(bf16[32,24,3584]{2,1,0:T(8,128)(2,1)} %bitcast.36), calls=%async_computation.1 | async-start | bytes 11010048 | tf_op jit(solution)/shard_map/all_to_all | solution.py:93

commit v6 on v5

--- a/solution.py
+++ b/solution.py
@@ -72,9 +72,8 @@
     part_back = contract_cols(got_cotangent, flat_b).reshape(total_rows, local_count, rank_width)
     pick_down = jnp.sum(part_down * onehot[:, :, None], axis=1)
     pick_back = jnp.sum(part_back * onehot[:, :, None], axis=1)
-    full = fsdp_sum(jnp.concatenate([pick_down, pick_back], axis=1))
-    full_down = full[:, :rank_width].astype(jnp.bfloat16)
-    full_back = full[:, rank_width:].astype(jnp.bfloat16)
+    full_back = fsdp_sum(pick_back).astype(jnp.bfloat16)
+    full_down = fsdp_sum(pick_down).astype(jnp.bfloat16)
     mask = onehot.astype(jnp.bfloat16)[:, :, None]
     down_rows = (mask * full_down[:, None, :]).reshape(total_rows, local_count * rank_width)
     back_rows = (mask * full_back[:, None, :]).reshape(total_rows, local_count * rank_width)

time: 359 us -> 344 us (0.958)
  waiting for transfers between devices: 295 us -> 276 us
  starting transfers between devices: 19.4 us -> 23.5 us
    all_to_all x1, waiting for transfers between devices: 111 us -> 86.8 us  [shards(): lax.all_to_all(returned, 'dp', split_axis=0, concat_axis=0, tiled=True)]
    ppermute x3 -> x6, waiting for transfers between devices: 21.5 us -> 25.8 us  [fsdp_sum(): x = x + lax.ppermute(x, 'fsdp', [(i, i ^ step) for i in range(n)])]
    ppermute x3 -> x6, starting transfers between devices: 2.85 us -> 6.99 us  [fsdp_sum(): x = x + lax.ppermute(x, 'fsdp', [(i, i ^ step) for i in range(n)])]
  transfers between devices with their start and end apart: 5 -> 8, of which waited for: 5 -> 8; matrix products, arithmetic and copies ran while one was open for 3% -> 5% of each run, Pallas kernels for 0% -> 0%
where the time goes in v6:
time: 344 us; the launch traced here: 340 us
  waiting for transfers between devices  276 us (80%)
  matrix products  36.8 us (11%)
  starting transfers between devices  23.5 us (7%)
    all_to_all x1, waiting for transfers between devices, shards(): recv = lax.all_to_all(send, 'dp', split_axis=0, concat_axis=0, tiled=True)  163 us
    all_to_all x1, waiting for transfers between devices, shards(): lax.all_to_all(returned, 'dp', split_axis=0, concat_axis=0, tiled=True)  86.8 us
    ppermute x6, waiting for transfers between devices, fsdp_sum(): x = x + lax.ppermute(x, 'fsdp', [(i, i ^ step) for i in range(n)])  25.8 us
    dot_general x2, matrix products, contract_rows(): lax.dot_general(left, right, (((0,), (0,)), ((), ())), preferred_element_...  10.4 us
    all_to_all x1, starting transfers between devices, shards(): recv = lax.all_to_all(send, 'dp', split_axis=0, concat_axis=0, tiled=True)  9.77 us
    dot_general x2, matrix products, contract_cols(): lax.dot_general(left, right, (((1,), (1,)), ((), ())), preferred_element_...  9.31 us
    ppermute x6, starting transfers between devices, fsdp_sum(): x = x + lax.ppermute(x, 'fsdp', [(i, i ^ step) for i in range(n)])  6.99 us
  transfers between devices with their start and end apart: 8, of which 8 were waited for; matrix products, arithmetic and copies ran while one was open for 5% of the time, Pallas kernels for 0%

profile of v6, /device:TPU:113, one launch (start us, length us, event | category | flops | bytes accessed | tf_op | source)
XLA Modules:
  0.0 339.7 jit_solution(2126757698155583905)
XLA Ops:
  0.6 0.8 and_select_fusion.1
  2.1 6.8 %convolution_convert_fusion = bf16[768,4736]{1,0:T(8,128)(2,1)} fusion(bf16[256,128]{1,0:T(8,128)(2,1)S(1)} %broadcast_in_dim.6, bf16[256,1024]{1,0:T(8,128)(2,1)} %param.6, bf16[256,3584]{1,0:T(8,128)(2,1)} %param.5, s32[768]{0:T(1024)S(1)} %select_n.25), kind=kOutput, calls=%fused_computation.1 | convolution fusion | flops 1873379328 | bytes 9702400 | tf_op jit(solution)/shard_map/dot_general | solution.py:60
  8.9 9.8 %all-to-all-start = ((bf16[32,24,4736]{2,1,0:T(8,128)(2,1)}), bf16[32,24,4736]{2,1,0:T(8,128)(2,1)}, u32[]{:S(2)}, u32[]{:S(2)}) async-start(bf16[32,24,4736]{2,1,0:T(8,128)(2,1)} %bitcast.35), calls=%async_computation | async-start | bytes 14548992 | tf_op jit(solution)/shard_map/all_to_all | solution.py:62
  18.7 163.1 %all-to-all-done = bf16[32,24,4736]{2,1,0:T(8,128)(2,1)} async-done(((bf16[32,24,4736]{2,1,0:T(8,128)(2,1)}), bf16[32,24,4736]{2,1,0:T(8,128)(2,1)}, u32[]{:S(2)}, u32[]{:S(2)}) %all-to-all-start) | async-done | bytes 7274528 | tf_op jit(solution)/shard_map/all_to_all | solution.py:62
  181.8 1.1 fusion.17
  183.0 2.6 multiply_reduce_fusion.1
  185.6 1.6 collective-permute-start
  187.2 1.1 collective-permute-done
  188.3 1.1 collective-permute-start.1
  189.4 5.1 %collective-permute-done.1 = f32[768,64]{0,1:T(8,128)S(1)} collective-permute-done((f32[768,64]{0,1:T(8,128)S(1)}, f32[768,64]{0,1:T(8,128)S(1)}, u32[]{:S(2)}, u32[]{:S(2)}) %collective-permute-start.1) | collective-permute-done | bytes 196640 | tf_op jit(solution)/shard_map/ppermute | solution.py:25
  194.7 6.7 %collective-permute-done.2 = f32[768,64]{0,1:T(8,128)S(1)} collective-permute-done((f32[768,64]{0,1:T(8,128)S(1)}, f32[768,64]{0,1:T(8,128)S(1)}, u32[]{:S(2)}, u32[]{:S(2)}) %collective-permute-start.2) | collective-permute-done | bytes 196640 | tf_op jit(solution)/shard_map/ppermute | solution.py:25
  201.4 4.9 %bitcast_convert_fusion = bf16[768,3584]{1,0:T(8,128)(2,1)} fusion(bf16[8,64,3584]{2,1,0:T(8,128)(2,1)S(1)} %copy-done.1, bf16[768,64]{0,1:T(8,128)(2,1)S(1)} %add_convert_fusion.1, bf16[768,8]{0,1:T(8,128)(2,1)S(1)} %get-tuple-element.3), kind=kOutput, calls=%fused_computation | convolution fusion | flops 2821718016 | bytes 9285632 | tf_op jit(solution)/shard_map/dot_general | solution.py:90
  206.3 6.8 %all-to-all-start.1 = ((bf16[32,24,3584]{2,1,0:T(8,128)(2,1)}), bf16[32,24,3584]{2,1,0:T(8,128)(2,1)}, u32[]{:S(2)}, u32[]{:S(2)}) async-start(bf16[32,24,3584]{2,1,0:T(8,128)(2,1)} %bitcast.36), calls=%async_computation.1 | async-start | bytes 11010048 | tf_op jit(solution)/shard_map/all_to_all | solution.py:92
  213.1 6.7 %multiply_reduce_fusion = f32[768,64]{0,1:T(8,128)S(1)} fusion(bf16[8,64,3584]{2,1,0:T(8,128)(2,1)} %param.8, bf16[768,4736]{1,0:T(8,128)(2,1)} %bitcast.2, f32[768,8]{0,1:T(8,128)S(1)} %get-tuple-element.4), kind=kOutput, calls=%fused_computation.12 | convolution fusion | flops 2819309568 | bytes 9396224 | tf_op jit(solution)/shard_map/dot_general | solution.py:14
  219.8 2.7 collective-permute-start.3
  222.5 1.1 collective-permute-done.3
  223.6 1.1 collective-permute-start.4
  224.9 5.0 %collective-permute-done.4 = f32[768,64]{0,1:T(8,128)S(1)} collective-permute-done((f32[768,64]{0,1:T(8,128)S(1)}, f32[768,64]{0,1:T(8,128)S(1)}, u32[]{:S(2)}, u32[]{:S(2)}) %collective-permute-start.4) | collective-permute-done | bytes 196640 | tf_op jit(solution)/shard_map/ppermute | solution.py:25
  229.9 0.3 collective-permute-start.5
  230.3 6.9 %collective-permute-done.5 = f32[768,64]{0,1:T(8,128)S(1)} collective-permute-done((f32[768,64]{0,1:T(8,128)S(1)}, f32[768,64]{0,1:T(8,128)S(1)}, u32[]{:S(2)}, u32[]{:S(2)}) %collective-permute-start.5) | collective-permute-done | bytes 196640 | tf_op jit(solution)/shard_map/ppermute | solution.py:25
  237.2 3.4 convolution_convert_fusion.3
  240.5 7.0 %convolution_convert_fusion.1 = bf16[8,64,3584]{2,1,0:T(8,128)(2,1)} fusion(bf16[768,4736]{1,0:T(8,128)(2,1)} %bitcast.2, bf16[768,64]{0,1:T(8,128)(2,1)S(1)} %add_convert_fusion.1, bf16[768,8]{0,1:T(8,128)(2,1)S(1)} %get-tuple-element.3), kind=kOutput, calls=%fused_computation.2 | convolution fusion | flops 2820800512 | bytes 9285632 | tf_op jit(solution)/shard_map/dot_general | solution.py:8
  247.5 86.8 %all-to-all-done.1 = bf16[32,24,3584]{2,1,0:T(8,128)(2,1)} async-done(((bf16[32,24,3584]{2,1,0:T(8,128)(2,1)}), bf16[32,24,3584]{2,1,0:T(8,128)(2,1)}, u32[]{:S(2)}, u32[]{:S(2)}) %all-to-all-start.1) | async-done | bytes 5505056 | tf_op jit(solution)/shard_map/all_to_all | solution.py:92
  334.3 5.4 %convolution_convert_fusion.2 = bf16[256,3584]{1,0:T(8,128)(2,1)} fusion(bf16[768,3584]{1,0:T(8,128)(2,1)} %bitcast.13, s32[256]{0:T(256)S(1)} %add_subtract_fusion), kind=kOutput, calls=%fused_computation.4 | convolution fusion | flops 1410400256 | bytes 7341056 | tf_op jit(solution)/shard_map/dot_general | solution.py:97
  (23 shorter events, 1.2 us)
Async XLA Ops:
  0.6 182.4 %copy-start = (bf16[8,64,1024]{2,1,0:T(8,128)(2,1)S(1)}, bf16[8,64,1024]{2,1,0:T(8,128)(2,1)}, u32[]{:S(2)}) copy-start(bf16[8,64,1024]{2,1,0:T(8,128)(2,1)} %param.9) | copy-start | bytes 3145732
  8.9 172.9 %all-to-all-start = ((bf16[32,24,4736]{2,1,0:T(8,128)(2,1)}), bf16[32,24,4736]{2,1,0:T(8,128)(2,1)}, u32[]{:S(2)}, u32[]{:S(2)}) async-start(bf16[32,24,4736]{2,1,0:T(8,128)(2,1)} %bitcast.35), calls=%async_computation | async-start | bytes 14548992 | tf_op jit(solution)/shard_map/all_to_all | solution.py:62
  183.0 18.4 %copy-start.1 = (bf16[8,64,3584]{2,1,0:T(8,128)(2,1)S(1)}, bf16[8,64,3584]{2,1,0:T(8,128)(2,1)}, u32[]{:S(2)}) copy-start(bf16[8,64,3584]{2,1,0:T(8,128)(2,1)} %param.8) | copy-start | bytes 11010052
  185.6 2.7 collective-permute-start
  188.3 6.2 %collective-permute-start.1 = (f32[768,64]{0,1:T(8,128)S(1)}, f32[768,64]{0,1:T(8,128)S(1)}, u32[]{:S(2)}, u32[]{:S(2)}) collective-permute-start(f32[768,64]{0,1:T(8,128)S(1)} %add.54), channel_id=1, source_target_pairs={{0,2},{1,3},{2,0},{3,1},{4,6},{5,7},{6,4},{7,5},{8,10},{9,11},{10,... | collective-permute-start | bytes 589832 | tf_op jit(solution)/shard_map/ppermute | solution.py:25
  194.5 6.8 %collective-permute-start.2 = (f32[768,64]{0,1:T(8,128)S(1)}, f32[768,64]{0,1:T(8,128)S(1)}, u32[]{:S(2)}, u32[]{:S(2)}) collective-permute-start(f32[768,64]{0,1:T(8,128)S(1)} %add.55), channel_id=1, source_target_pairs={{0,4},{1,5},{2,6},{3,7},{4,0},{5,1},{6,2},{7,3},{8,12},{9,13},{10,... | collective-permute-start | bytes 589832 | tf_op jit(solution)/shard_map/ppermute | solution.py:25
  206.3 128.0 %all-to-all-start.1 = ((bf16[32,24,3584]{2,1,0:T(8,128)(2,1)}), bf16[32,24,3584]{2,1,0:T(8,128)(2,1)}, u32[]{:S(2)}, u32[]{:S(2)}) async-start(bf16[32,24,3584]{2,1,0:T(8,128)(2,1)} %bitcast.36), calls=%async_computation.1 | async-start | bytes 11010048 | tf_op jit(solution)/shard_map/all_to_all | solution.py:92
  219.8 3.8 %collective-permute-start.3 = (f32[768,64]{0,1:T(8,128)S(1)}, f32[768,64]{0,1:T(8,128)S(1)}, u32[]{:S(2)}, u32[]{:S(2)}) collective-permute-start(f32[768,64]{0,1:T(8,128)S(1)} %multiply_reduce_fusion), channel_id=1, source_target_pairs={{0,1},{1,0},{2,3},{3,2},{4,5},{5,4},{6,7},{7,6},{8,9},{9,8},{10,11... | collective-permute-start | bytes 589832 | tf_op jit(solution)/shard_map/ppermute | solution.py:25
  223.6 6.3 %collective-permute-start.4 = (f32[768,64]{0,1:T(8,128)S(1)}, f32[768,64]{0,1:T(8,128)S(1)}, u32[]{:S(2)}, u32[]{:S(2)}) collective-permute-start(f32[768,64]{0,1:T(8,128)S(1)} %add.57), channel_id=1, source_target_pairs={{0,2},{1,3},{2,0},{3,1},{4,6},{5,7},{6,4},{7,5},{8,10},{9,11},{10,... | collective-permute-start | bytes 589832 | tf_op jit(solution)/shard_map/ppermute | solution.py:25
  229.9 7.2 %collective-permute-start.5 = (f32[768,64]{0,1:T(8,128)S(1)}, f32[768,64]{0,1:T(8,128)S(1)}, u32[]{:S(2)}, u32[]{:S(2)}) collective-permute-start(f32[768,64]{0,1:T(8,128)S(1)} %add.58), channel_id=1, source_target_pairs={{0,4},{1,5},{2,6},{3,7},{4,0},{5,1},{6,2},{7,3},{8,12},{9,13},{10,... | collective-permute-start | bytes 589832 | tf_op jit(solution)/shard_map/ppermute | solution.py:25

commit v7 on v6

--- a/solution.py
+++ b/solution.py
@@ -46,9 +46,8 @@
     wanted = jnp.where(usable, starts[:, None] + slot_index[None, :], -1).reshape(total_rows)
     pick = (wanted[:, None] == token_index[None, :]).astype(jnp.bfloat16)
     id_width = 128
-    table = jnp.concatenate(
+    small = jnp.concatenate(
         [
-            hidden,
             cotangent,
             jnp.broadcast_to(
                 (region_ids % local_count + 1).astype(jnp.bfloat16)[:, None],
@@ -57,13 +56,16 @@
         ],
         axis=-1,
     )
-    send = jnp.dot(pick, table, preferred_element_type=jnp.float32).astype(jnp.bfloat16)
-    send = send.reshape(owner_count, capacity, hidden_width + model_width + id_width)
-    recv = lax.all_to_all(send, "dp", split_axis=0, concat_axis=0, tiled=True)
-    recv = recv.reshape(total_rows, hidden_width + model_width + id_width)
-    got_hidden = recv[:, :hidden_width]
-    got_cotangent = recv[:, hidden_width : hidden_width + model_width]
-    got_local = recv[:, hidden_width + model_width] - 1
+    send_small = jnp.dot(pick, small, preferred_element_type=jnp.float32).astype(jnp.bfloat16)
+    send_small = send_small.reshape(owner_count, capacity, model_width + id_width)
+    recv_small = lax.all_to_all(send_small, "dp", split_axis=0, concat_axis=0, tiled=True)
+    recv_small = recv_small.reshape(total_rows, model_width + id_width)
+    send_hidden = jnp.dot(pick, hidden, preferred_element_type=jnp.float32).astype(jnp.bfloat16)
+    send_hidden = send_hidden.reshape(owner_count, capacity, hidden_width)
+    got_hidden = lax.all_to_all(send_hidden, "dp", split_axis=0, concat_axis=0, tiled=True)
+    got_hidden = got_hidden.reshape(total_rows, hidden_width)
+    got_cotangent = recv_small[:, :model_width]
+    got_local = recv_small[:, model_width] - 1
     local_ids = jnp.arange(local_count).astype(jnp.bfloat16)
     onehot = (got_local[:, None] == local_ids[None, :]).astype(jnp.float32)
     flat_a = adapter_a.reshape(local_count * rank_width, hidden_width)

time: 344 us -> 326 us (0.948)
  waiting for transfers between devices: 276 us -> 250 us
  starting transfers between devices: 23.5 us -> 32.9 us
    all_to_all x1 -> x2, waiting for transfers between devices: 163 us -> 133 us  [the longest x1 95.5 us: shards(): lax.all_to_all(send_hidden, 'dp', split_axis=0, concat_axis=0, tiled=True)]
    all_to_all x1, waiting for transfers between devices: 86.8 us -> 97 us  [shards(): lax.all_to_all(returned, 'dp', split_axis=0, concat_axis=0, tiled=True)]
    all_to_all x1 -> x2, starting transfers between devices: 9.77 us -> 16.8 us  [the longest x1 9.77 us: shards(): lax.all_to_all(send_small, 'dp', split_axis=0, concat_axis=0, tiled=True)]
    ppermute x6, waiting for transfers between devices: 25.8 us -> 19.2 us  [fsdp_sum(): x = x + lax.ppermute(x, 'fsdp', [(i, i ^ step) for i in range(n)])]
    all_to_all x1, starting transfers between devices: 6.79 us -> 10.5 us  [shards(): lax.all_to_all(returned, 'dp', split_axis=0, concat_axis=0, tiled=True)]
    dot_general x1 -> x2, matrix products: 6.82 us -> 6.97 us  [the longest x1 3.99 us: shards(): jnp.dot(pick, hidden, preferred_element_type=jnp.float32)]
  transfers between devices with their start and end apart: 8 -> 9, of which waited for: 8 -> 8; matrix products, arithmetic and copies ran while one was open for 5% -> 9% of each run, Pallas kernels for 0% -> 0%
where the time goes in v7:
time: 326 us; the launch traced here: 323 us
  waiting for transfers between devices  250 us (77%)
  matrix products  37 us (11%)
  starting transfers between devices  32.9 us (10%)
    all_to_all x1, waiting for transfers between devices, shards(): lax.all_to_all(returned, 'dp', split_axis=0, concat_axis=0, tiled=True)  97 us
    all_to_all x1, waiting for transfers between devices, shards(): lax.all_to_all(send_hidden, 'dp', split_axis=0, concat_axis=0, tiled=True)  95.5 us
    all_to_all x1, waiting for transfers between devices, shards(): lax.all_to_all(send_small, 'dp', split_axis=0, concat_axis=0, tiled=True)  37.9 us
    ppermute x6, waiting for transfers between devices, fsdp_sum(): x = x + lax.ppermute(x, 'fsdp', [(i, i ^ step) for i in range(n)])  19.2 us
    all_to_all x1, starting transfers between devices, shards(): lax.all_to_all(returned, 'dp', split_axis=0, concat_axis=0, tiled=True)  10.5 us
    dot_general x2, matrix products, contract_rows(): lax.dot_general(left, right, (((0,), (0,)), ((), ())), preferred_element_...  10.4 us
    all_to_all x1, starting transfers between devices, shards(): lax.all_to_all(send_small, 'dp', split_axis=0, concat_axis=0, tiled=True)  9.77 us
    dot_general x2, matrix products, contract_cols(): lax.dot_general(left, right, (((1,), (1,)), ((), ())), preferred_element_...  9.32 us
  transfers between devices with their start and end apart: 9, of which 8 were waited for; matrix products, arithmetic and copies ran while one was open for 9% of the time, Pallas kernels for 0%

profile of v7, /device:TPU:113, one launch (start us, length us, event | category | flops | bytes accessed | tf_op | source)
XLA Modules:
  0.0 323.2 jit_solution(9213636483424097386)
XLA Ops:
  2.1 3.0 convolution_convert_fusion.3
  5.1 9.8 %all-to-all-start = ((bf16[32,24,1152]{2,1,0:T(8,128)(2,1)}), bf16[32,24,1152]{2,1,0:T(8,128)(2,1)}, u32[]{:S(2)}, u32[]{:S(2)}) async-start(bf16[32,24,1152]{2,1,0:T(8,128)(2,1)} %bitcast.37), calls=%async_computation | async-start | bytes 3538944 | tf_op jit(solution)/shard_map/all_to_all | solution.py:61
  14.9 4.0 %convolution_convert_fusion = bf16[768,3584]{1,0:T(8,128)(2,1)} fusion(bf16[256,3584]{1,0:T(8,128)(2,1)S(1)} %copy-done, s32[768]{0:T(1024)S(1)} %select_n.25), kind=kOutput, calls=%fused_computation.1 | convolution fusion | flops 1412235264 | bytes 7343104 | tf_op jit(solution)/shard_map/dot_general | solution.py:63
  18.9 37.9 %all-to-all-done = bf16[32,24,1152]{2,1,0:T(8,128)(2,1)} async-done(((bf16[32,24,1152]{2,1,0:T(8,128)(2,1)}), bf16[32,24,1152]{2,1,0:T(8,128)(2,1)}, u32[]{:S(2)}, u32[]{:S(2)}) %all-to-all-start) | async-done | bytes 1769504 | tf_op jit(solution)/shard_map/all_to_all | solution.py:61
  56.8 7.0 %all-to-all-start.1 = ((bf16[32,24,3584]{2,1,0:T(8,128)(2,1)}), bf16[32,24,3584]{2,1,0:T(8,128)(2,1)}, u32[]{:S(2)}, u32[]{:S(2)}) async-start(bf16[32,24,3584]{2,1,0:T(8,128)(2,1)} %bitcast.36), calls=%async_computation.1 | async-start | bytes 11010048 | tf_op jit(solution)/shard_map/all_to_all | solution.py:65
  63.8 1.1 fusion.15
  65.0 2.6 multiply_reduce_fusion.1
  67.6 1.8 collective-permute-start
  69.4 1.1 collective-permute-done
  70.5 1.1 collective-permute-start.1
  71.6 5.2 %collective-permute-done.1 = f32[768,64]{0,1:T(8,128)S(1)} collective-permute-done((f32[768,64]{0,1:T(8,128)S(1)}, f32[768,64]{0,1:T(8,128)S(1)}, u32[]{:S(2)}, u32[]{:S(2)}) %collective-permute-start.1) | collective-permute-done | bytes 196640 | tf_op jit(solution)/shard_map/ppermute | solution.py:25
  77.0 6.9 %collective-permute-done.2 = f32[768,64]{0,1:T(8,128)S(1)} collective-permute-done((f32[768,64]{0,1:T(8,128)S(1)}, f32[768,64]{0,1:T(8,128)S(1)}, u32[]{:S(2)}, u32[]{:S(2)}) %collective-permute-start.2) | collective-permute-done | bytes 196640 | tf_op jit(solution)/shard_map/ppermute | solution.py:25
  83.9 4.9 %bitcast_convert_fusion = bf16[768,3584]{1,0:T(8,128)(2,1)} fusion(bf16[8,64,3584]{2,1,0:T(8,128)(2,1)S(1)} %copy-done.1, bf16[768,64]{0,1:T(8,128)(2,1)S(1)} %add_convert_fusion.1, bf16[768,8]{0,1:T(8,128)(2,1)S(1)} %get-tuple-element.3), kind=kOutput, calls=%fused_computation | convolution fusion | flops 2821718016 | bytes 9285632 | tf_op jit(solution)/shard_map/dot_general | solution.py:92
  88.8 95.5 %all-to-all-done.1 = bf16[32,24,3584]{2,1,0:T(8,128)(2,1)} async-done(((bf16[32,24,3584]{2,1,0:T(8,128)(2,1)}), bf16[32,24,3584]{2,1,0:T(8,128)(2,1)}, u32[]{:S(2)}, u32[]{:S(2)}) %all-to-all-start.1) | async-done | bytes 5505056 | tf_op jit(solution)/shard_map/all_to_all | solution.py:65
  184.3 10.5 %all-to-all-start.2 = ((bf16[32,24,3584]{2,1,0:T(8,128)(2,1)}), bf16[32,24,3584]{2,1,0:T(8,128)(2,1)}, u32[]{:S(2)}, u32[]{:S(2)}) async-start(bf16[32,24,3584]{2,1,0:T(8,128)(2,1)} %bitcast.38), calls=%async_computation.2 | async-start | bytes 11010048 | tf_op jit(solution)/shard_map/all_to_all | solution.py:94
  194.8 6.7 %multiply_reduce_fusion = f32[768,64]{0,1:T(8,128)S(1)} fusion(bf16[768,3584,1]{1,0,2:T(8,128)(2,1)} %bitcast.9, bf16[8,64,3584]{2,1,0:T(8,128)(2,1)} %param.8, f32[768,8]{0,1:T(8,128)S(1)} %get-tuple-element.4), kind=kOutput, calls=%fused_computation.6 | convolution fusion | flops 2819309568 | bytes 9396224 | tf_op jit(solution)/shard_map/dot_general | solution.py:14
  201.5 1.1 collective-permute-start.3
  202.8 0.9 collective-permute-done.3
  203.8 1.1 collective-permute-start.4
  204.8 5.2 %collective-permute-done.4 = f32[768,64]{0,1:T(8,128)S(1)} collective-permute-done((f32[768,64]{0,1:T(8,128)S(1)}, f32[768,64]{0,1:T(8,128)S(1)}, u32[]{:S(2)}, u32[]{:S(2)}) %collective-permute-start.4) | collective-permute-done | bytes 196640 | tf_op jit(solution)/shard_map/ppermute | solution.py:25
  210.4 7.0 %convolution_convert_fusion.1 = bf16[8,64,3584]{2,1,0:T(8,128)(2,1)} fusion(bf16[768,3584,1]{1,0,2:T(8,128)(2,1)} %bitcast.9, bf16[768,64]{0,1:T(8,128)(2,1)S(1)} %add_convert_fusion.1, bf16[768,8]{0,1:T(8,128)(2,1)S(1)} %get-tuple-element.3), kind=kOutput, calls=%fused_computation.2 | convolution fusion | flops 2820800512 | bytes 9285632 | tf_op jit(solution)/shard_map/dot_general | solution.py:8
  217.4 3.4 %convolution_convert_fusion.4 = bf16[8,64,1024]{2,1,0:T(8,128)(2,1)} fusion(bf16[768,1152]{1,0:T(8,128)(2,1)} %bitcast.2, bf16[768,64]{0,1:T(8,128)(2,1)S(1)} %add_convert_fusion, bf16[768,8]{0,1:T(8,128)(2,1)S(1)} %get-tuple-element.3), kind=kOutput, calls=%fused_computation.8 | convolution fusion | flops 806223872 | bytes 2732032 | tf_op jit(solution)/shard_map/dot_general | solution.py:8
  220.8 97.0 %all-to-all-done.2 = bf16[32,24,3584]{2,1,0:T(8,128)(2,1)} async-done(((bf16[32,24,3584]{2,1,0:T(8,128)(2,1)}), bf16[32,24,3584]{2,1,0:T(8,128)(2,1)}, u32[]{:S(2)}, u32[]{:S(2)}) %all-to-all-start.2) | async-done | bytes 5505056 | tf_op jit(solution)/shard_map/all_to_all | solution.py:94
  317.8 5.4 %convolution_convert_fusion.2 = bf16[256,3584]{1,0:T(8,128)(2,1)} fusion(bf16[768,3584]{1,0:T(8,128)(2,1)} %bitcast.16, s32[256]{0:T(256)S(1)} %add_subtract_fusion), kind=kOutput, calls=%fused_computation.3 | convolution fusion | flops 1410400256 | bytes 7341056 | tf_op jit(solution)/shard_map/dot_general | solution.py:99
  (28 shorter events, 2.4 us)
Async XLA Ops:
  0.6 14.3 %copy-start = (bf16[256,3584]{1,0:T(8,128)(2,1)S(1)}, bf16[256,3584]{1,0:T(8,128)(2,1)}, u32[]{:S(2)}) copy-start(bf16[256,3584]{1,0:T(8,128)(2,1)} %param.5) | copy-start | bytes 5505028
  5.1 51.7 %all-to-all-start = ((bf16[32,24,1152]{2,1,0:T(8,128)(2,1)}), bf16[32,24,1152]{2,1,0:T(8,128)(2,1)}, u32[]{:S(2)}, u32[]{:S(2)}) async-start(bf16[32,24,1152]{2,1,0:T(8,128)(2,1)} %bitcast.37), calls=%async_computation | async-start | bytes 3538944 | tf_op jit(solution)/shard_map/all_to_all | solution.py:61
  56.8 8.2 %copy-start.2 = (bf16[8,64,1024]{2,1,0:T(8,128)(2,1)S(1)}, bf16[8,64,1024]{2,1,0:T(8,128)(2,1)}, u32[]{:S(2)}) copy-start(bf16[8,64,1024]{2,1,0:T(8,128)(2,1)} %param.9) | copy-start | bytes 3145732
  56.8 127.5 %all-to-all-start.1 = ((bf16[32,24,3584]{2,1,0:T(8,128)(2,1)}), bf16[32,24,3584]{2,1,0:T(8,128)(2,1)}, u32[]{:S(2)}, u32[]{:S(2)}) async-start(bf16[32,24,3584]{2,1,0:T(8,128)(2,1)} %bitcast.36), calls=%async_computation.1 | async-start | bytes 11010048 | tf_op jit(solution)/shard_map/all_to_all | solution.py:65
  65.0 18.9 %copy-start.1 = (bf16[8,64,3584]{2,1,0:T(8,128)(2,1)S(1)}, bf16[8,64,3584]{2,1,0:T(8,128)(2,1)}, u32[]{:S(2)}) copy-start(bf16[8,64,3584]{2,1,0:T(8,128)(2,1)} %param.8) | copy-start | bytes 11010052
  67.6 2.9 collective-permute-start
  70.5 6.3 %collective-permute-start.1 = (f32[768,64]{0,1:T(8,128)S(1)}, f32[768,64]{0,1:T(8,128)S(1)}, u32[]{:S(2)}, u32[]{:S(2)}) collective-permute-start(f32[768,64]{0,1:T(8,128)S(1)} %add.54), channel_id=1, source_target_pairs={{0,2},{1,3},{2,0},{3,1},{4,6},{5,7},{6,4},{7,5},{8,10},{9,11},{10,... | collective-permute-start | bytes 589832 | tf_op jit(solution)/shard_map/ppermute | solution.py:25
  76.8 7.0 %collective-permute-start.2 = (f32[768,64]{0,1:T(8,128)S(1)}, f32[768,64]{0,1:T(8,128)S(1)}, u32[]{:S(2)}, u32[]{:S(2)}) collective-permute-start(f32[768,64]{0,1:T(8,128)S(1)} %add.55), channel_id=1, source_target_pairs={{0,4},{1,5},{2,6},{3,7},{4,0},{5,1},{6,2},{7,3},{8,12},{9,13},{10,... | collective-permute-start | bytes 589832 | tf_op jit(solution)/shard_map/ppermute | solution.py:25
  184.3 133.5 %all-to-all-start.2 = ((bf16[32,24,3584]{2,1,0:T(8,128)(2,1)}), bf16[32,24,3584]{2,1,0:T(8,128)(2,1)}, u32[]{:S(2)}, u32[]{:S(2)}) async-start(bf16[32,24,3584]{2,1,0:T(8,128)(2,1)} %bitcast.38), calls=%async_computation.2 | async-start | bytes 11010048 | tf_op jit(solution)/shard_map/all_to_all | solution.py:94
  201.5 2.2 collective-permute-start.3
  203.8 6.3 %collective-permute-start.4 = (f32[768,64]{0,1:T(8,128)S(1)}, f32[768,64]{0,1:T(8,128)S(1)}, u32[]{:S(2)}, u32[]{:S(2)}) collective-permute-start(f32[768,64]{0,1:T(8,128)S(1)} %add.57), channel_id=1, source_target_pairs={{0,2},{1,3},{2,0},{3,1},{4,6},{5,7},{6,4},{7,5},{8,10},{9,11},{10,... | collective-permute-start | bytes 589832 | tf_op jit(solution)/shard_map/ppermute | solution.py:25
  210.1 7.3 %collective-permute-start.5 = (f32[768,64]{0,1:T(8,128)S(1)}, f32[768,64]{0,1:T(8,128)S(1)}, u32[]{:S(2)}, u32[]{:S(2)}) collective-permute-start(f32[768,64]{0,1:T(8,128)S(1)} %add.58), channel_id=1, source_target_pairs={{0,4},{1,5},{2,6},{3,7},{4,0},{5,1},{6,2},{7,3},{8,12},{9,13},{10,... | collective-permute-start | bytes 589832 | tf_op jit(solution)/shard_map/ppermute | solution.py:25
